TPU v7x, 128 devices: a whole 4x4x4 slice. The times are simulated.
128 devices in a mesh: dp: 16 (over y, z), cls: 8 (over x, core).
Axes of the slice: x: 4, y: 4, z: 4, core: 2. Of those that a mesh axis runs over, the one named last changes fastest.
Arguments:
- particles: bfloat16 [16384, 2, 64, 128], P(('dp', 'cls')), may hold values from -128 to 128
- references: bfloat16 [200, 2, 64, 128], P('cls', None, 'dp'), may hold values from -6 to 6
- class_index: int32 [16384, 8], P(('dp', 'cls')), may hold values from 0 to 199, all different within a row
- rotation_index: int32 [16384, 8], P(('dp', 'cls')), may hold values from 0 to 35
- defocus_group: int32 [16384], P(('dp', 'cls')), may hold values from 0 to 127
- log_prior: float32 [16384, 8], P(('dp', 'cls')), may hold values from -3 to 400
- ctf_table: float32 [128, 64], replicated, may hold values from -1 to 1
Outputs:
- new_references: float32 [200, 2, 64, 128], P('cls', None, 'dp')
- responsibilities: float32 [16384, 8], P(('dp', 'cls'))
Inputs may be any that keep to these rules, and one draw needn't show every extreme that they name: `class_index`: each row names 8 different classes; every class is named by some row.
All inputs are finite; a program needn't handle non-finite values.
Results may differ from a plain program's by a relative error of at most 0.0029.
Values may be sent and summed in bfloat16 or wider, within the bound.
No kernel may reach another device: no remote copies, remote signals or barrier semaphores. Data moves between devices by JAX's collectives and lax.ppermute only.
A program may use at most 128 MiB of HBM per device.

v0:
```python
import math

import jax
import jax.numpy as jnp
from jax import lax
from jax.sharding import PartitionSpec as P

NROT = 36


SCORE_SCALE = 0.0025
REGULARIZER = 1.0


def phase_tables(rotations, harmonics):
    turns = (
        jnp.arange(rotations, dtype=jnp.int32)[:, None]
        * jnp.arange(harmonics, dtype=jnp.int32)[None, :]
        % rotations
    )
    angle = turns.astype(jnp.float32) * (2.0 * math.pi / rotations)
    return (jnp.cos(angle), jnp.sin(angle))


def body(particles, references, class_index, rotation_index, defocus_group, log_prior, ctf_table):
    partial_refs = lax.all_gather(references, "cls", axis=0, tiled=True)
    all_refs = lax.all_gather(partial_refs, "dp", axis=2, tiled=True)
    total_rows = particles.shape[0]
    cycle_count = particles.shape[2]
    harmonics = particles.shape[3]
    classes = all_refs.shape[0]
    top_count = class_index.shape[1]
    groups = ctf_table.shape[0]
    feature_count = 2 * cycle_count * harmonics
    flat_refs = all_refs.reshape(classes, feature_count)
    group_hot = (defocus_group[:, None] == jnp.arange(groups, dtype=jnp.int32)[None, :]).astype(
        jnp.float32
    )
    ctf_all = jnp.dot(group_hot, ctf_table, precision=lax.Precision.HIGHEST)
    cosine_table, sine_table = phase_tables(NROT, harmonics)
    per_block = min(total_rows, 32)
    num_blocks = total_rows // per_block
    pair_rows = per_block * top_count

    def one_block(running, inputs):
        images, class_blk, rot_blk, ctf_rows, prior_blk = inputs
        rot_hot = (
            rot_blk.reshape(pair_rows, 1) == jnp.arange(NROT, dtype=jnp.int32)[None, :]
        ).astype(jnp.float32)
        cos_rows = jnp.dot(rot_hot, cosine_table, precision=lax.Precision.HIGHEST).reshape(
            per_block, top_count, 1, harmonics
        )
        sin_rows = jnp.dot(rot_hot, sine_table, precision=lax.Precision.HIGHEST).reshape(
            per_block, top_count, 1, harmonics
        )
        scale = ctf_rows[:, None, :, None]
        real_part = images[:, None, 0, :, :]
        imag_part = images[:, None, 1, :, :]
        rot_real = scale * (real_part * cos_rows - imag_part * sin_rows)
        rot_imag = scale * (real_part * sin_rows + imag_part * cos_rows)
        ref_rows = jnp.take(flat_refs, class_blk.reshape(-1), axis=0).reshape(
            per_block, top_count, 2, cycle_count, harmonics
        )
        intersection = jnp.sum(
            rot_real * ref_rows[:, :, 0] + rot_imag * ref_rows[:, :, 1], axis=(2, 3)
        )
        weights = jax.nn.softmax(prior_blk + SCORE_SCALE * intersection, axis=-1)
        contribution = jnp.stack(
            [weights[:, :, None, None] * rot_real, weights[:, :, None, None] * rot_imag], axis=2
        ).astype(jnp.bfloat16)
        contribution = contribution.reshape(pair_rows, feature_count)
        class_hot = class_blk.reshape(pair_rows, 1) == jnp.arange(classes, dtype=jnp.int32)[None, :]
        class_sums = running[0] + jnp.einsum(
            "qc,qf->cf",
            class_hot.astype(jnp.bfloat16),
            contribution,
            preferred_element_type=jnp.float32,
        )
        squared = (weights[:, :, None] * (ctf_rows * ctf_rows)[:, None, :]).reshape(
            pair_rows, cycle_count
        )
        class_weight = running[1] + jnp.einsum(
            "qc,qr->cr", class_hot.astype(jnp.float32), squared, precision=lax.Precision.HIGHEST
        )
        return ((class_sums, class_weight), weights)

    start = (
        jnp.zeros((classes, feature_count), jnp.float32),
        jnp.zeros((classes, cycle_count), jnp.float32),
    )
    inputs = (
        particles.reshape(num_blocks, per_block, 2, cycle_count, harmonics),
        class_index.reshape(num_blocks, per_block, top_count),
        rotation_index.reshape(num_blocks, per_block, top_count),
        ctf_all.reshape(num_blocks, per_block, cycle_count),
        log_prior.reshape(num_blocks, per_block, top_count),
    )
    (class_sums, class_weight), weights = lax.scan(one_block, start, inputs)
    class_sums = class_sums.reshape(classes, 2, cycle_count, harmonics)
    cycle_sums, cycle_weight = (
        lax.psum_scatter(class_sums, "dp", scatter_dimension=2, tiled=True),
        lax.psum_scatter(class_weight, "dp", scatter_dimension=1, tiled=True),
    )
    owned_sums, owned_weight = (
        lax.psum_scatter(cycle_sums, "cls", scatter_dimension=0, tiled=True),
        lax.psum_scatter(cycle_weight, "cls", scatter_dimension=0, tiled=True),
    )
    new_references = owned_sums / (owned_weight[:, None, :, None] + REGULARIZER)
    return (new_references, weights.reshape(total_rows, top_count))


def solution(mesh):
    in_specs = (
        P(("dp", "cls"), None, None, None),
        P("cls", None, "dp", None),
        P(("dp", "cls"), None),
        P(("dp", "cls"), None),
        P(("dp", "cls")),
        P(("dp", "cls"), None),
        P(),
    )
    out_specs = (P("cls", None, "dp", None), P(("dp", "cls"), None))
    return jax.shard_map(body, mesh=mesh, in_specs=in_specs, out_specs=out_specs, check_vma=False)
```

profile of v0, /device:TPU:1, one launch (start us, length us, event | category | flops | bytes accessed | tf_op | source)
XLA Modules:
  0.0 653.5 jit_solution(10197735293390590924)
XLA Ops:
  7.2 14.9 %all_gather.6 = bf16[200,2,4,128]{3,2,1,0:T(4,128)(2,1)S(1)} all-gather(bf16[25,2,4,128]{3,2,1,0:T(4,128)(2,1)} %param.10), channel_id=1, replica_groups=mesh['dp'=16,'cls'=8] {'cls'}, dimensions={0}, use_global_device_ids=true | all-gather | bytes 460800 | tf_op jit(solution)/shard_map/all_gather | solution.py:26
  26.3 60.6 %all-gather.2.cloned.1.call-done = bf16[200,2,64,128]{3,0,1,2:T(8,128)(2,1)} async-done(((bf16[200,2,4,128]{3,0,1,2:T(8,128)(2,1)}), bf16[200,2,64,128]{3,0,1,2:T(8,128)(2,1)}) %all-gather.2.cloned.1.call-update) | async-done | bytes 6553616 | tf_op jit(solution)/shard_map/all_gather | solution.py:27
  91.6 8.8 %copy.57 = bf16[25,8,128,128]{3,1,2,0:T(8,128)(2,1)} copy(bf16[25,8,128,128]{3,2,1,0:T(8,128)(2,1)S(1)} %bitcast.112) | data formatting | bytes 13107200
  100.4 329.2 %while.15 = (s32[]{:T(128)}, f32[200,16384]{1,0:T(8,128)}, f32[200,64]{0,1:T(8,128)S(1)}, f32[4,32,8]{2,1,0:T(8,128)S(1)}, s32[4,32,8]{2,1,0:T(8,128)S(1)}, /*in...) while((s32[]{:T(128)}, f32[200,16384]{1,0:T(8,128)}, ...), condition=%wide.region_4.5_spmd.clone, body=%wide.region_0.4_spmd.clone.sunk | while | flops 1815602688 | bytes 129737040 | solution.py:98
  115.1 20.1 %gather_fusion = bf16[256,16384]{1,0:T(8,128)(2,1)} fusion(bf16[200,16384]{1,0:T(8,128)(2,1)} %get-tuple-element.296, s32[1024]{0:T(1024)S(1)} %pad_clamp_fusion.2), kind=kCustom, calls=%fused_computation.clone.clone.1 | custom fusion | bytes 16778240 | tf_op jit(solution)/shard_map/while/body/eval_jaxpr/jit(_take)/gather | solution.py:61
  145.0 8.4 %fusion.61 = f32[32,8]{1,0:T(8,128)S(1)} fusion(bf16[32,8,2,64,128]{4,1,3,2,0:T(8,128)(2,1)} %broadcast_select_fusion.2, f32[32,8,128]{2,1,0:T(8,128)S(1)} %convolution_bitcast_fusion.4, f32[32,64,128]{2,1,0:T(8,128)S(1)} %get-tuple-element.251, f32[32,8,128]{2,1,0:T(8,128)S(1)} %convolution_bitcast_fusion.5, ...), kind=kLoop, calls=%fused_computation.7.clone.1 | loop fusion | flops 29359872 | bytes 10757120 | tf_op jit(solution)/shard_map/while/body/eval_jaxpr/reduce_sum | solution.py:64
  167.2 13.3 %convert_element_type.58 = bf16[256,16384]{1,0:T(8,128)(2,1)} reshape(bf16[32,8,2,64,128]{4,3,2,1,0:T(8,128)(2,1)} %pad_maximum_fusion.2) | data formatting | bytes 16777216 | tf_op jit(solution)/shard_map/while/body/eval_jaxpr/convert_element_type | solution.py:70
  180.5 10.2 %convolution_add_fusion.4 = f32[200,16384]{1,0:T(8,128)} fusion(bf16[256,16384]{1,0:T(8,128)(2,1)} %convert_element_type.58, f32[200,16384]{1,0:T(8,128)} %get-tuple-element.276, pred[]{:T(512)S(6)} %compare.3, s32[256]{0:T(256)S(1)} %eq.122), kind=kOutput, calls=%fused_computation.3.clone.1 | convolution fusion | flops 1684326400 | bytes 34604032 | tf_op jit(solution)/shard_map/while/body/eval_jaxpr/qc,qf->cf/dot_general | solution.py:73
  190.9 20.1 %gather_fusion = bf16[256,16384]{1,0:T(8,128)(2,1)} fusion(bf16[200,16384]{1,0:T(8,128)(2,1)} %get-tuple-element.296, s32[1024]{0:T(1024)S(1)} %pad_clamp_fusion.2), kind=kCustom, calls=%fused_computation.clone.clone.1 | custom fusion | bytes 16778240 | tf_op jit(solution)/shard_map/while/body/eval_jaxpr/jit(_take)/gather | solution.py:61
  243.0 13.3 %convert_element_type.58 = bf16[256,16384]{1,0:T(8,128)(2,1)} reshape(bf16[32,8,2,64,128]{4,3,2,1,0:T(8,128)(2,1)} %pad_maximum_fusion.2) | data formatting | bytes 16777216 | tf_op jit(solution)/shard_map/while/body/eval_jaxpr/convert_element_type | solution.py:70
  256.3 14.0 %convolution_add_fusion.4 = f32[200,16384]{1,0:T(8,128)} fusion(bf16[256,16384]{1,0:T(8,128)(2,1)} %convert_element_type.58, f32[200,16384]{1,0:T(8,128)} %get-tuple-element.276, pred[]{:T(512)S(6)} %compare.3, s32[256]{0:T(256)S(1)} %eq.122), kind=kOutput, calls=%fused_computation.3.clone.1 | convolution fusion | flops 1684326400 | bytes 34604032 | tf_op jit(solution)/shard_map/while/body/eval_jaxpr/qc,qf->cf/dot_general | solution.py:73
  270.5 20.1 %gather_fusion = bf16[256,16384]{1,0:T(8,128)(2,1)} fusion(bf16[200,16384]{1,0:T(8,128)(2,1)} %get-tuple-element.296, s32[1024]{0:T(1024)S(1)} %pad_clamp_fusion.2), kind=kCustom, calls=%fused_computation.clone.clone.1 | custom fusion | bytes 16778240 | tf_op jit(solution)/shard_map/while/body/eval_jaxpr/jit(_take)/gather | solution.py:61
  300.4 8.4 %fusion.61 = f32[32,8]{1,0:T(8,128)S(1)} fusion(bf16[32,8,2,64,128]{4,1,3,2,0:T(8,128)(2,1)} %broadcast_select_fusion.2, f32[32,8,128]{2,1,0:T(8,128)S(1)} %convolution_bitcast_fusion.4, f32[32,64,128]{2,1,0:T(8,128)S(1)} %get-tuple-element.251, f32[32,8,128]{2,1,0:T(8,128)S(1)} %convolution_bitcast_fusion.5, ...), kind=kLoop, calls=%fused_computation.7.clone.1 | loop fusion | flops 29359872 | bytes 10757120 | tf_op jit(solution)/shard_map/while/body/eval_jaxpr/reduce_sum | solution.py:64
  322.5 13.3 %convert_element_type.58 = bf16[256,16384]{1,0:T(8,128)(2,1)} reshape(bf16[32,8,2,64,128]{4,3,2,1,0:T(8,128)(2,1)} %pad_maximum_fusion.2) | data formatting | bytes 16777216 | tf_op jit(solution)/shard_map/while/body/eval_jaxpr/convert_element_type | solution.py:70
  335.9 14.0 %convolution_add_fusion.4 = f32[200,16384]{1,0:T(8,128)} fusion(bf16[256,16384]{1,0:T(8,128)(2,1)} %convert_element_type.58, f32[200,16384]{1,0:T(8,128)} %get-tuple-element.276, pred[]{:T(512)S(6)} %compare.3, s32[256]{0:T(256)S(1)} %eq.122), kind=kOutput, calls=%fused_computation.3.clone.1 | convolution fusion | flops 1684326400 | bytes 34604032 | tf_op jit(solution)/shard_map/while/body/eval_jaxpr/qc,qf->cf/dot_general | solution.py:73
  350.0 20.1 %gather_fusion = bf16[256,16384]{1,0:T(8,128)(2,1)} fusion(bf16[200,16384]{1,0:T(8,128)(2,1)} %get-tuple-element.296, s32[1024]{0:T(1024)S(1)} %pad_clamp_fusion.2), kind=kCustom, calls=%fused_computation.clone.clone.1 | custom fusion | bytes 16778240 | tf_op jit(solution)/shard_map/while/body/eval_jaxpr/jit(_take)/gather | solution.py:61
  379.9 8.4 %fusion.61 = f32[32,8]{1,0:T(8,128)S(1)} fusion(bf16[32,8,2,64,128]{4,1,3,2,0:T(8,128)(2,1)} %broadcast_select_fusion.2, f32[32,8,128]{2,1,0:T(8,128)S(1)} %convolution_bitcast_fusion.4, f32[32,64,128]{2,1,0:T(8,128)S(1)} %get-tuple-element.251, f32[32,8,128]{2,1,0:T(8,128)S(1)} %convolution_bitcast_fusion.5, ...), kind=kLoop, calls=%fused_computation.7.clone.1 | loop fusion | flops 29359872 | bytes 10757120 | tf_op jit(solution)/shard_map/while/body/eval_jaxpr/reduce_sum | solution.py:64
  402.1 13.3 %convert_element_type.58 = bf16[256,16384]{1,0:T(8,128)(2,1)} reshape(bf16[32,8,2,64,128]{4,3,2,1,0:T(8,128)(2,1)} %pad_maximum_fusion.2) | data formatting | bytes 16777216 | tf_op jit(solution)/shard_map/while/body/eval_jaxpr/convert_element_type | solution.py:70
  415.4 14.0 %convolution_add_fusion.4 = f32[200,16384]{1,0:T(8,128)} fusion(bf16[256,16384]{1,0:T(8,128)(2,1)} %convert_element_type.58, f32[200,16384]{1,0:T(8,128)} %get-tuple-element.276, pred[]{:T(512)S(6)} %compare.3, s32[256]{0:T(256)S(1)} %eq.122), kind=kOutput, calls=%fused_computation.3.clone.1 | convolution fusion | flops 1684326400 | bytes 34604032 | tf_op jit(solution)/shard_map/while/body/eval_jaxpr/qc,qf->cf/dot_general | solution.py:73
  429.6 11.9 %copy.54 = f32[25,8,128,128]{3,2,1,0:T(8,128)} copy(f32[25,8,128,128]{3,1,2,0:T(8,128)} %bitcast.110) | data formatting | bytes 26214400
  441.5 17.0 %copy.41 = f32[200,2,64,128]{3,0,1,2:T(8,128)} copy(f32[200,2,64,128]{3,2,1,0:T(8,128)} %bitcast.111) | data formatting | bytes 26214400 | tf_op jit(solution)/shard_map/reshape | solution.py:99
  458.5 95.8 %reduce-scatter.3.cloned.1.call-done = f32[200,2,4,128]{3,0,1,2:T(8,128)} async-done(((f32[200,2,64,128]{3,0,1,2:T(8,128)}), f32[200,2,4,128]{3,0,1,2:T(8,128)}) %reduce-scatter.3.cloned.1.call-update) | async-done | bytes 819216 | tf_op jit(solution)/shard_map/reduce_scatter | solution.py:101
  559.2 58.1 %all-reduce.1 = f32[200,64]{0,1:T(8,128)S(1)} all-reduce(f32[200,64]{0,1:T(8,128)S(1)} %get-tuple-element.67), channel_id=4, replica_groups=mesh['dp'=16,'cls'=8] {'dp'}, use_global_device_ids=true, to_apply=%region_7.8.clone | all-reduce | flops 12800 | bytes 102400
  617.4 26.8 %all-reduce.2 = f32[200,4]{0,1:T(4,128)S(1)} all-reduce(f32[200,4]{0,1:T(4,128)S(1)} %constant_dynamic-slice_fusion.4), channel_id=5, replica_groups=mesh['dp'=16,'cls'=8] {'cls'}, use_global_device_ids=true, to_apply=%region_8.9.clone | all-reduce | flops 800 | bytes 6400
  (221 shorter events, 117.7 us)
Async XLA Ops:
  7.2 18.3 %copy-start = (f32[128,64]{0,1:T(8,128)S(1)}, f32[128,64]{0,1:T(8,128)}, u32[]{:S(2)}) copy-start(f32[128,64]{0,1:T(8,128)} %param.15) | copy-start | bytes 98308
  7.2 79.8 %all-gather.2.cloned.1.call-start = ((), (), s32[]{:S(2)}) async-start(), calls=%async_computation.1 | async-start | bytes 6963200 | tf_op jit(solution)/shard_map/all_gather | solution.py:27
  23.0 531.4 %reduce-scatter.3.cloned.1.call-start = ((), (), s32[]{:S(2)}) async-start(), calls=%async_computation.2 | async-start | bytes 13926400 | tf_op jit(solution)/shard_map/reduce_scatter | solution.py:101
  115.0 20.2 %copy-start.4 = (s32[4,32,8]{2,1,0:T(8,128)}, s32[4,32,8]{2,1,0:T(8,128)S(1)}, u32[]{:S(2)}) copy-start(s32[4,32,8]{2,1,0:T(8,128)S(1)} %get-tuple-element.291) | copy-start | bytes 12292 | tf_op jit(solution)/shard_map/while
  115.0 29.3 %copy-start.6 = (s32[4,32,8]{2,1,0:T(8,128)}, s32[4,32,8]{2,1,0:T(8,128)S(1)}, u32[]{:S(2)}) copy-start(s32[4,32,8]{2,1,0:T(8,128)S(1)} %get-tuple-element.295) | copy-start | bytes 12292 | tf_op jit(solution)/shard_map/while
  115.0 30.0 %copy-start.2 = (f32[4,32,64]{2,1,0:T(8,128)}, f32[4,32,64]{2,1,0:T(8,128)S(1)}, u32[]{:S(2)}) copy-start(f32[4,32,64]{2,1,0:T(8,128)S(1)} %get-tuple-element.293) | copy-start | bytes 98308 | tf_op jit(solution)/shard_map/while
  190.8 20.2 %copy-start.4 = (s32[4,32,8]{2,1,0:T(8,128)}, s32[4,32,8]{2,1,0:T(8,128)S(1)}, u32[]{:S(2)}) copy-start(s32[4,32,8]{2,1,0:T(8,128)S(1)} %get-tuple-element.291) | copy-start | bytes 12292 | tf_op jit(solution)/shard_map/while
  190.8 29.3 %copy-start.6 = (s32[4,32,8]{2,1,0:T(8,128)}, s32[4,32,8]{2,1,0:T(8,128)S(1)}, u32[]{:S(2)}) copy-start(s32[4,32,8]{2,1,0:T(8,128)S(1)} %get-tuple-element.295) | copy-start | bytes 12292 | tf_op jit(solution)/shard_map/while
  190.8 30.0 %copy-start.2 = (f32[4,32,64]{2,1,0:T(8,128)}, f32[4,32,64]{2,1,0:T(8,128)S(1)}, u32[]{:S(2)}) copy-start(f32[4,32,64]{2,1,0:T(8,128)S(1)} %get-tuple-element.293) | copy-start | bytes 98308 | tf_op jit(solution)/shard_map/while
  256.3 14.0 %copy-start.9 = (f32[200,64]{0,1:T(8,128)S(1)}, f32[200,64]{0,1:T(8,128)}, u32[]{:S(2)}) copy-start(f32[200,64]{0,1:T(8,128)} %copy-done.8) | copy-start | bytes 153604 | tf_op jit(solution)/shard_map/while
  256.3 14.0 %copy-start.11 = (f32[4,32,8]{2,1,0:T(8,128)S(1)}, f32[4,32,8]{2,1,0:T(8,128)}, u32[]{:S(2)}) copy-start(f32[4,32,8]{2,1,0:T(8,128)} %copy-done.10) | copy-start | bytes 12292 | tf_op jit(solution)/shard_map/while
  270.3 20.2 %copy-start.4 = (s32[4,32,8]{2,1,0:T(8,128)}, s32[4,32,8]{2,1,0:T(8,128)S(1)}, u32[]{:S(2)}) copy-start(s32[4,32,8]{2,1,0:T(8,128)S(1)} %get-tuple-element.291) | copy-start | bytes 12292 | tf_op jit(solution)/shard_map/while
  270.3 29.3 %copy-start.6 = (s32[4,32,8]{2,1,0:T(8,128)}, s32[4,32,8]{2,1,0:T(8,128)S(1)}, u32[]{:S(2)}) copy-start(s32[4,32,8]{2,1,0:T(8,128)S(1)} %get-tuple-element.295) | copy-start | bytes 12292 | tf_op jit(solution)/shard_map/while
  270.3 30.0 %copy-start.2 = (f32[4,32,64]{2,1,0:T(8,128)}, f32[4,32,64]{2,1,0:T(8,128)S(1)}, u32[]{:S(2)}) copy-start(f32[4,32,64]{2,1,0:T(8,128)S(1)} %get-tuple-element.293) | copy-start | bytes 98308 | tf_op jit(solution)/shard_map/while
  335.8 14.0 %copy-start.9 = (f32[200,64]{0,1:T(8,128)S(1)}, f32[200,64]{0,1:T(8,128)}, u32[]{:S(2)}) copy-start(f32[200,64]{0,1:T(8,128)} %copy-done.8) | copy-start | bytes 153604 | tf_op jit(solution)/shard_map/while
  335.8 14.0 %copy-start.11 = (f32[4,32,8]{2,1,0:T(8,128)S(1)}, f32[4,32,8]{2,1,0:T(8,128)}, u32[]{:S(2)}) copy-start(f32[4,32,8]{2,1,0:T(8,128)} %copy-done.10) | copy-start | bytes 12292 | tf_op jit(solution)/shard_map/while
  349.9 20.2 %copy-start.4 = (s32[4,32,8]{2,1,0:T(8,128)}, s32[4,32,8]{2,1,0:T(8,128)S(1)}, u32[]{:S(2)}) copy-start(s32[4,32,8]{2,1,0:T(8,128)S(1)} %get-tuple-element.291) | copy-start | bytes 12292 | tf_op jit(solution)/shard_map/while
  349.9 29.3 %copy-start.6 = (s32[4,32,8]{2,1,0:T(8,128)}, s32[4,32,8]{2,1,0:T(8,128)S(1)}, u32[]{:S(2)}) copy-start(s32[4,32,8]{2,1,0:T(8,128)S(1)} %get-tuple-element.295) | copy-start | bytes 12292 | tf_op jit(solution)/shard_map/while
  349.9 30.0 %copy-start.2 = (f32[4,32,64]{2,1,0:T(8,128)}, f32[4,32,64]{2,1,0:T(8,128)S(1)}, u32[]{:S(2)}) copy-start(f32[4,32,64]{2,1,0:T(8,128)S(1)} %get-tuple-element.293) | copy-start | bytes 98308 | tf_op jit(solution)/shard_map/while
  415.4 14.0 %copy-start.11 = (f32[4,32,8]{2,1,0:T(8,128)S(1)}, f32[4,32,8]{2,1,0:T(8,128)}, u32[]{:S(2)}) copy-start(f32[4,32,8]{2,1,0:T(8,128)} %copy-done.10) | copy-start | bytes 12292 | tf_op jit(solution)/shard_map/while
  441.5 205.2 %copy-start.1 = (f32[128,64]{0,1:T(8,128)S(1)}, f32[128,64]{0,1:T(8,128)}, u32[]{:S(2)}) copy-start(f32[128,64]{0,1:T(8,128)} %param.15) | copy-start | bytes 98308
  458.5 98.3 %copy-start.13 = (u32[128]{0:T(128)S(1)}, u32[128]{0:T(128)}, u32[]{:S(2)}) copy-start(u32[128]{0:T(128)} %constant.66) | copy-start | bytes 1540
  458.5 98.9 %copy-start.12 = (u32[128]{0:T(128)S(1)}, u32[128]{0:T(128)}, u32[]{:S(2)}) copy-start(u32[128]{0:T(128)} %constant.62) | copy-start | bytes 1540
  458.5 186.5 %all-reduce.5.cloned.1.call-start = ((), (), s32[]{:S(2)}) async-start(), calls=%async_computation.3 | async-start | bytes 1638400
  (23 other events, 197.6 us)
Sparse Core Ops, SparseCore 0:
  23.1 63.8 all-gather.1
  458.6 95.7 reduce-scatter.2
  556.9 58.1 all-reduce.4
where the time goes:
time: 663 us; the launch traced here: 654 us
  local copies, waits for them, and re-layouts  194 us (29%)
  waiting for transfers between devices  157 us (24%)
  other arithmetic  115 us (17%)
  blocking collectives  99.8 us (15%)
  matrix products  56.8 us (9%)
  loops' own time  15.7 us (2%)
  between operations  15.5 us (2%)
    reduce_scatter x1, waiting for transfers between devices, body(): lax.psum_scatter(class_sums, 'dp', scatter_dimension=2, tiled=True)  95.8 us
    unnamed x2, blocking collectives  84.9 us
    gather x4, local copies, waits for them, and re-layouts, one_block(): jnp.take(flat_refs, class_blk.reshape(-1), axis=0)  80.2 us
    all_gather x1, waiting for transfers between devices, body(): all_refs = lax.all_gather(partial_refs, 'dp', axis=2, tiled=True)  60.6 us
    convert_element_type x4, local copies, waits for them, and re-layouts, one_block(): contribution = jnp.stack([weights[:, :, None, None] * rot_real, weights[:...  53.2 us
    dot_general x4, matrix products, one_block(): jnp.einsum('qc,qf->cf', class_hot.astype(jnp.bfloat16), contribution, pre...  52.1 us
    reduce_sum x4, other arithmetic, one_block(): jnp.sum(rot_real * ref_rows[:, :, 0] + rot_imag * ref_rows[:, :, 1], axis...  33.6 us
    select_n x8, other arithmetic, one_block(): jnp.take(flat_refs, class_blk.reshape(-1), axis=0)  30.1 us
  transfers between devices with their start and end apart: 3, of which 2 were waited for; matrix products, arithmetic and copies ran while one was open for 1% of the time, Pallas kernels for 0%

commit v1 on v0

v1 whole, which is shorter than its diff:
```python
import math

import jax
import jax.numpy as jnp
import numpy as np
from jax import lax
from jax.experimental import pallas as pl
from jax.experimental.pallas import tpu as pltpu
from jax.sharding import PartitionSpec as P

NROT = 36
SCORE_SCALE = 0.0025
REGULARIZER = 1.0

F32 = jnp.float32
BF16 = jnp.bfloat16
LANES = 128
INDEX_ROWS = 32
VMEM_LIMIT = 56 * 1024 * 1024


def split3_np(x):
    hi = x.astype(jnp.bfloat16)
    rest = x - hi.astype(np.float32)
    mid = rest.astype(jnp.bfloat16)
    low = (rest - mid.astype(np.float32)).astype(jnp.bfloat16)
    return hi, mid, low


def rounded(x):
    return lax.reduce_precision(x, exponent_bits=8, mantissa_bits=7)


def split3(x):
    hi = rounded(x)
    rest = x - hi
    mid = rounded(rest)
    low = rounded(rest - mid)
    return hi.astype(BF16), mid.astype(BF16), low.astype(BF16)


def phase_table(harmonics):
    turns = (np.arange(NROT)[:, None] * np.arange(harmonics)[None, :]) % NROT
    angle = turns.astype(np.float32) * np.float32(2.0 * math.pi / NROT)
    both = np.concatenate([np.cos(angle), np.sin(angle)], axis=1).astype(np.float32)
    stacked = np.concatenate(split3_np(both), axis=0)
    pad = np.zeros((128 - 3 * NROT, 2 * harmonics), stacked.dtype)
    return np.concatenate([stacked, pad], axis=0)


def cut_kernel(share, x_ref, index_ref, out_ref, wide):
    step = pl.program_id(0)
    block, parts, cycles, lanes = x_ref.shape
    owners = out_ref.shape[0]
    total = block * pl.num_programs(0)
    rows = parts * cycles
    wide[...] = x_ref[...].astype(F32).reshape(block * rows, lanes)
    for owner in range(owners):
        for part in range(parts):
            for i in range(share):
                row = part * cycles + owner * share + i
                piece = wide[pl.ds(row, block, stride=rows), :]
                slab = part * share + i
                out_ref[owner, pl.ds(pl.multiple_of(slab * 128 + step * block, block), block), :] = piece.astype(BF16)

    @pl.when(step == 0)
    def _():
        for owner in range(owners):
            out_ref[owner, 2 * share * 128 :, :] = index_ref[...]


def cut_particles(particles, index_rows, owners):
    count, parts, cycles, lanes = particles.shape
    share = cycles // owners
    block = 32
    out_rows = 2 * share * count + INDEX_ROWS
    return pl.pallas_call(
        lambda *refs: cut_kernel(share, *refs),
        name="cut",
        grid=(count // block,),
        in_specs=[
            pl.BlockSpec((block, parts, cycles, lanes), lambda s: (s, 0, 0, 0)),
            pl.BlockSpec((INDEX_ROWS, lanes), lambda s: (0, 0)),
        ],
        out_specs=pl.BlockSpec((owners, out_rows, lanes), lambda s: (0, 0, 0)),
        out_shape=jax.ShapeDtypeStruct((owners, out_rows, lanes), BF16),
        scratch_shapes=[pltpu.VMEM((block * parts * cycles, lanes), F32)],
        compiler_params=pltpu.CompilerParams(vmem_limit_bytes=VMEM_LIMIT),
    )(particles, index_rows)


def lane_iota(rows, width):
    return lax.broadcasted_iota(jnp.int32, (rows, width), 1)


def transposed_index(rows):
    wide = jnp.concatenate([rows.astype(F32), jnp.zeros((LANES - INDEX_ROWS, LANES), F32)], axis=0)
    return wide.T


def scaled_particles(x_ref, columns, ctf_table, scaled, slabs):
    group = columns[:, 16:17]
    lanes = lane_iota(LANES, 384)
    hot = jnp.where(group == (lanes % 128).astype(F32), 1.0, 0.0).astype(BF16)
    ctf = jnp.dot(hot, ctf_table[...], preferred_element_type=F32)
    half = slabs // 2
    for slab in range(slabs):
        r = slab % half
        scaled[slab] = x_ref[0, slab * 128 : (slab + 1) * 128, :].astype(F32) * ctf[:, r * 128 : (r + 1) * 128]
    return hot


def rotation(columns, j, phases):
    lanes = lane_iota(LANES, 128)
    within = jnp.where(lanes < 3 * NROT, lanes % NROT, -1).astype(F32)
    hot = jnp.where(columns[:, 8 + j : 9 + j] == within, 1.0, 0.0).astype(BF16)
    both = jnp.dot(hot, phases[...], preferred_element_type=F32)
    return both[:, :128], both[:, 128:]


def score_kernel(slabs, top, x_ref, refs_ref, ctf_table, phases, out_ref, table, scaled):
    half = slabs // 2

    @pl.when(pl.program_id(0) == 0)
    def _():
        for dev in range(refs_ref.shape[0]):
            for slab in range(slabs):
                table[dev * 32 : (dev + 1) * 32, slab * 128 : (slab + 1) * 128] = refs_ref[dev, slab]

    columns = transposed_index(x_ref[0, slabs * 128 :, :])
    scaled_particles(x_ref, columns, ctf_table, scaled, slabs)
    classes = lane_iota(LANES, 256).astype(F32)
    lanes = lane_iota(LANES, LANES)
    scores = jnp.zeros((LANES, LANES), F32)
    for j in range(top):
        hot = jnp.where(columns[:, j : j + 1] == classes, 1.0, 0.0).astype(BF16)
        picked = jnp.dot(hot, table[...], preferred_element_type=F32)
        cosine, sine = rotation(columns, j, phases)
        even = odd = None
        for r in range(half):
            ref_re = picked[:, r * 128 : (r + 1) * 128]
            ref_im = picked[:, (half + r) * 128 : (half + r + 1) * 128]
            re, im = scaled[r], scaled[half + r]
            a = re * ref_re + im * ref_im
            b = re * ref_im - im * ref_re
            even = a if even is None else even + a
            odd = b if odd is None else odd + b
        total = jnp.sum(cosine * even + sine * odd, axis=1, keepdims=True)
        scores = jnp.where(lanes == j, total, scores)
    out_ref[0] = (SCORE_SCALE * scores).T[:top]


def partial_scores(moved, refs, ctf_table, phases, slabs, top):
    sources, rows, lanes = moved.shape
    whole = lambda a: pl.BlockSpec(a.shape, lambda s, n=a.ndim: (0,) * n)
    return pl.pallas_call(
        lambda *args: score_kernel(slabs, top, *args),
        name="score",
        grid=(sources,),
        in_specs=[pl.BlockSpec((1, rows, lanes), lambda s: (s, 0, 0)), whole(refs), whole(ctf_table), whole(phases)],
        out_specs=pl.BlockSpec((1, top, lanes), lambda s: (s, 0, 0)),
        out_shape=jax.ShapeDtypeStruct((sources, top, lanes), F32),
        scratch_shapes=[pltpu.VMEM((256, slabs * 128), BF16), pltpu.VMEM((slabs, 128, lanes), F32)],
        compiler_params=pltpu.CompilerParams(vmem_limit_bytes=VMEM_LIMIT),
    )(moved, refs, ctf_table, phases)


def sum_kernel(slabs, top, x_ref, partial_ref, ctf_table, ctf_lanes, phases, weight_ref, out_ref, scaled, contribution, hots, total, norm):
    half = slabs // 2
    step = pl.program_id(0)

    @pl.when(step == 0)
    def _():
        total[...] = jnp.zeros_like(total)
        norm[...] = jnp.zeros_like(norm)

    score = partial_ref[0, 0]
    for source in range(1, partial_ref.shape[0]):
        score = score + partial_ref[source, 0]
    raised = jnp.exp(score - jnp.max(score, axis=0, keepdims=True))
    weight = raised / jnp.sum(raised, axis=0, keepdims=True)
    weight_ref[0] = weight
    weight_columns = jnp.concatenate([weight, jnp.zeros((LANES - top, LANES), F32)], axis=0).T

    index_rows = x_ref[0, slabs * 128 :, :].astype(F32)
    columns = transposed_index(index_rows)
    group_hot = scaled_particles(x_ref, columns, ctf_table, scaled, slabs)
    classes = lax.broadcasted_iota(jnp.int32, (256, LANES), 0).astype(F32)
    spread = jnp.zeros((256, LANES), F32)
    for j in range(top):
        cosine, sine = rotation(columns, j, phases)
        w = weight_columns[:, j : j + 1]
        wc = w * cosine
        ws = w * sine
        for r in range(half):
            re, im = scaled[r], scaled[half + r]
            contribution[j * 128 : (j + 1) * 128, r * 128 : (r + 1) * 128] = (re * wc - im * ws).astype(BF16)
            contribution[j * 128 : (j + 1) * 128, (half + r) * 128 : (half + r + 1) * 128] = (re * ws + im * wc).astype(BF16)
        mine = index_rows[j : j + 1, :] == classes
        hots[:, j * 128 : (j + 1) * 128] = jnp.where(mine, 1.0, 0.0).astype(BF16)
        spread = jnp.where(mine, weight[j : j + 1, :], spread)
    total[...] += jnp.dot(hots[...], contribution[...], preferred_element_type=F32)
    ctf = jnp.dot(group_hot, ctf_lanes[...], preferred_element_type=F32)
    norm[...] += jnp.dot(spread, ctf * ctf, preferred_element_type=F32, precision=lax.Precision.HIGHEST)

    @pl.when(step == pl.num_programs(0) - 1)
    def _():
        n = norm[...]
        hi = n.astype(BF16)
        rest = n - hi.astype(F32)
        mid = rest.astype(BF16)
        low = (rest - mid.astype(F32)).astype(BF16)
        coded = jnp.where(
            lane_iota(256, LANES) < half,
            hi.astype(F32),
            jnp.where(
                lane_iota(256, LANES) < 2 * half,
                pltpu.roll(mid.astype(F32), half, 1),
                pltpu.roll(low.astype(F32), 2 * half, 1),
            ),
        ).astype(BF16)
        for dev in range(out_ref.shape[0]):
            rows = slice(dev * 32, (dev + 1) * 32)
            for slab in range(slabs):
                out_ref[dev, slab] = total[rows, slab * 128 : (slab + 1) * 128].astype(BF16)
            out_ref[dev, slabs] = coded[rows]


def weighted_sums(moved, partials, ctf_table, ctf_lanes, phases, slabs, top, owners):
    sources, rows, lanes = moved.shape
    whole = lambda a: pl.BlockSpec(a.shape, lambda s, n=a.ndim: (0,) * n)
    return pl.pallas_call(
        lambda *args: sum_kernel(slabs, top, *args),
        name="sums",
        grid=(sources,),
        in_specs=[
            pl.BlockSpec((1, rows, lanes), lambda s: (s, 0, 0)),
            pl.BlockSpec((sources, 1, top, lanes), lambda s: (0, s, 0, 0)),
            whole(ctf_table),
            whole(ctf_lanes),
            whole(phases),
        ],
        out_specs=[
            pl.BlockSpec((1, top, lanes), lambda s: (s, 0, 0)),
            pl.BlockSpec((owners, slabs + 1, 32, lanes), lambda s: (0, 0, 0, 0)),
        ],
        out_shape=[
            jax.ShapeDtypeStruct((sources, top, lanes), F32),
            jax.ShapeDtypeStruct((owners, slabs + 1, 32, lanes), BF16),
        ],
        scratch_shapes=[
            pltpu.VMEM((slabs, 128, lanes), F32),
            pltpu.VMEM((top * 128, slabs * 128), BF16),
            pltpu.VMEM((256, top * 128), BF16),
            pltpu.VMEM((256, slabs * 128), F32),
            pltpu.VMEM((256, lanes), F32),
        ],
        compiler_params=pltpu.CompilerParams(vmem_limit_bytes=VMEM_LIMIT),
    )(moved, partials, ctf_table, ctf_lanes, phases)


def finish_kernel(slabs, owned, parts_ref, out_ref):
    half = slabs // 2

    def gathered(slab):
        value = parts_ref[0, slab].astype(F32)
        for source in range(1, parts_ref.shape[0]):
            value = value + parts_ref[source, slab].astype(F32)
        return value

    coded = gathered(slabs)
    norm = coded + pltpu.roll(coded, LANES - half, 1) + pltpu.roll(coded, LANES - 2 * half, 1) + REGULARIZER
    for r in range(half):
        scale = 1.0 / norm[:, r : r + 1]
        for part in range(2):
            out_ref[:, part, r, :] = (gathered(part * half + r) * scale)[:owned]


def finish(parts, owned, slabs):
    return pl.pallas_call(
        lambda *args: finish_kernel(slabs, owned, *args),
        name="finish",
        out_shape=jax.ShapeDtypeStruct((owned, 2, slabs // 2, LANES), F32),
        compiler_params=pltpu.CompilerParams(vmem_limit_bytes=VMEM_LIMIT),
    )(parts)


def body(particles, references, class_index, rotation_index, defocus_group, log_prior, ctf_table):
    count, _, cycles, harmonics = particles.shape
    owned, _, share, _ = references.shape
    top = class_index.shape[1]
    owners = cycles // share
    slabs = 2 * share
    me = lax.axis_index("dp")

    padded = class_index + (32 - owned) * (class_index // owned)
    index_rows = jnp.concatenate(
        [padded, rotation_index, defocus_group[:, None], jnp.zeros((count, INDEX_ROWS - 2 * top - 1), jnp.int32)], axis=1
    )
    index_rows = index_rows.T.astype(BF16)
    send = cut_particles(particles, index_rows, owners)
    moved = lax.all_to_all(send, "dp", 0, 0)

    own_refs = jnp.pad(references.transpose(1, 2, 0, 3).reshape(slabs, owned, harmonics), ((0, 0), (0, 32 - owned), (0, 0)))
    refs = lax.all_gather(own_refs, "cls", axis=0)

    ctf = lax.dynamic_slice(ctf_table, (0, me * share), (ctf_table.shape[0], share))
    ctf_parts = jnp.concatenate(split3(ctf), axis=0)
    ctf_wide = jnp.broadcast_to(ctf_parts[:, :, None], ctf_parts.shape + (LANES,)).reshape(-1, share * LANES)
    ctf_lanes = jnp.pad(ctf_parts, ((0, 0), (0, LANES - share)))
    phases = jnp.asarray(phase_table(harmonics))

    partial = partial_scores(moved, refs, ctf_wide, phases, slabs, top)
    mine = (jnp.arange(owners) == me)[:, None, None]
    partial = partial + jnp.where(mine, log_prior.T[None], 0.0)
    partials = lax.all_to_all(jnp.broadcast_to(partial[None], (owners,) + partial.shape), "dp", 0, 0)

    weights, sums = weighted_sums(moved, partials, ctf_wide, ctf_lanes, phases, slabs, top, refs.shape[0])
    parts = lax.all_to_all(sums, "cls", 0, 0)
    new_references = finish(parts, owned, slabs)
    own_weights = lax.dynamic_index_in_dim(weights, me, 0, keepdims=False).T
    return new_references, own_weights


def solution(mesh):
    in_specs = (
        P(("dp", "cls"), None, None, None),
        P("cls", None, "dp", None),
        P(("dp", "cls"), None),
        P(("dp", "cls"), None),
        P(("dp", "cls")),
        P(("dp", "cls"), None),
        P(),
    )
    out_specs = (P("cls", None, "dp", None), P(("dp", "cls"), None))
    return jax.shard_map(body, mesh=mesh, in_specs=in_specs, out_specs=out_specs, check_vma=False)
```

time: 663 us -> 200 us (0.30); the launches traced: 654 us -> 199 us
  local copies, waits for them, and re-layouts: 194 us -> 6.37 us
  other arithmetic: 115 us -> 4.36 us
  waiting for transfers between devices: 157 us -> 70.9 us
  blocking collectives: 99.8 us -> 15.3 us
  Pallas kernels: 0 us -> 76.7 us
  matrix products: 56.8 us -> 0 us
  starting transfers between devices: 0.12 us -> 25.1 us
  loops' own time: 15.7 us -> 0 us
  between operations: 15.5 us -> 0.72 us
    reduce_scatter x1 -> x0, waiting for transfers between devices: 95.8 us -> none  [body(): lax.psum_scatter(class_sums, 'dp', scatter_dimension=2, tiled=True)]
    unnamed x2 -> x0, blocking collectives: 84.9 us -> none
    gather x4 -> x0, local copies, waits for them, and re-layouts: 80.2 us -> none  [one_block(): jnp.take(flat_refs, class_blk.reshape(-1), axis=0)]
    pallas_call x0 -> x4, Pallas kernels: none -> 76.7 us  [the longest x1 39.4 us: weighted_sums(): pl.pallas_call(lambda *args: sum_kernel(slabs, top, *args), name='sums',...]
    all_to_all x0 -> x3, waiting for transfers between devices: none -> 70.9 us  [the longest x1 48 us: body(): moved = lax.all_to_all(send, 'dp', 0, 0)]
    all_gather x1 -> x0, waiting for transfers between devices: 60.6 us -> none  [body(): all_refs = lax.all_gather(partial_refs, 'dp', axis=2, tiled=True)]
    dot_general x17 -> x0, matrix products: 56.8 us -> none  [the longest x4 52.1 us: one_block(): jnp.einsum('qc,qf->cf', class_hot.astype(jnp.bfloat16), contribution, pre...]
    convert_element_type x4 -> x0, local copies, waits for them, and re-layouts: 53.2 us -> none  [one_block(): contribution = jnp.stack([weights[:, :, None, None] * rot_real, weights[:...]
  transfers between devices with their start and end apart: 3 -> 3, of which waited for: 2 -> 3; matrix products, arithmetic and copies ran while one was open for 1% -> 2% of each run, Pallas kernels for 0% -> 0%
where the time goes in v1:
time: 200 us; the launch traced here: 199 us
  Pallas kernels  76.7 us (38%)
  waiting for transfers between devices  70.9 us (35%)
  starting transfers between devices  25.1 us (13%)
  blocking collectives  15.3 us (8%)
  local copies, waits for them, and re-layouts  6.37 us (3%)
  other arithmetic  4.36 us (2%)
    all_to_all x1, waiting for transfers between devices, body(): moved = lax.all_to_all(send, 'dp', 0, 0)  48 us
    pallas_call x1, Pallas kernels, weighted_sums(): pl.pallas_call(lambda *args: sum_kernel(slabs, top, *args), name='sums',...  39.4 us
    pallas_call x1, Pallas kernels, partial_scores(): pl.pallas_call(lambda *args: score_kernel(slabs, top, *args), name='score...  26.9 us
    all_gather x1, blocking collectives, body(): refs = lax.all_gather(own_refs, 'cls', axis=0)  15.3 us
    all_to_all x1, waiting for transfers between devices, body(): lax.all_to_all(jnp.broadcast_to(partial[None], (owners,) + partial.shape)...  14 us
    all_to_all x1, waiting for transfers between devices, body(): parts = lax.all_to_all(sums, 'cls', 0, 0)  8.91 us
    all_to_all x1, starting transfers between devices, body(): moved = lax.all_to_all(send, 'dp', 0, 0)  8.77 us
    all_to_all x1, starting transfers between devices, body(): lax.all_to_all(jnp.broadcast_to(partial[None], (owners,) + partial.shape)...  8.71 us
  transfers between devices with their start and end apart: 3, of which 3 were waited for; matrix products, arithmetic and copies ran while one was open for 2% of the time, Pallas kernels for 0%

profile of v1, /device:TPU:1, one launch (start us, length us, event | category | flops | bytes accessed | tf_op | source)
XLA Modules:
  0.0 199.4 jit_solution(15470030323696011445)
XLA Ops:
  0.6 0.7 convert_bitcast_fusion
  1.3 0.7 convert.13
  2.0 0.7 fusion.2
  2.8 0.7 maximum_bitcast_fusion.refs_1_
  3.4 8.5 %cut.1 = bf16[16,1056,128]{2,1,0:T(8,128)(2,1)} custom-call(bf16[128,2,64,128]{3,2,1,0:T(8,128)(2,1)} %refs_0_.1, bf16[32,128]{1,0:T(8,128)(2,1)} %maximum_bitcast_fusion.refs_1_), custom_call_target="tpu_custom_call" | custom-call | tf_op jit(solution)/shard_map/cut/pallas_call | solution.py:77
  11.9 8.8 %all-to-all-start = ((bf16[16,1056,128]{2,1,0:T(8,128)(2,1)}), bf16[16,1056,128]{2,1,0:T(8,128)(2,1)}, u32[]{:S(2)}, u32[]{:S(2)}) async-start(bf16[16,1056,128]{2,1,0:T(8,128)(2,1)} %cut.1), calls=%async_computation | async-start | bytes 8650752 | tf_op jit(solution)/shard_map/all_to_all | solution.py:302
  20.8 0.7 reduce-precision_convert_fusion.1
  21.7 0.5 broadcast_in_dim.43
  22.1 0.8 copy.17
  23.0 15.3 %all-gather = bf16[64,32,128]{2,1,0:T(8,128)(2,1)} all-gather(bf16[8,32,128]{2,1,0:T(8,128)(2,1)S(1)} %pad.8), channel_id=2, replica_groups=mesh['dp'=16,'cls'=8] {'cls'}, dimensions={0}, use_global_device_ids=true | all-gather | bytes 589824 | tf_op jit(solution)/shard_map/all_gather | solution.py:305
  38.3 48.0 %all-to-all-done.args_0_ = bf16[16,1056,128]{2,1,0:T(8,128)(2,1)} async-done(((bf16[16,1056,128]{2,1,0:T(8,128)(2,1)}), bf16[16,1056,128]{2,1,0:T(8,128)(2,1)}, u32[]{:S(2)}, u32[]{:S(2)}) %all-to-all-start) | async-done | bytes 4325408 | tf_op jit(solution)/shard_map/all_to_all | solution.py:302
  86.2 26.9 %score.1 = f32[16,8,128]{2,1,0:T(8,128)} custom-call(bf16[16,1056,128]{2,1,0:T(8,128)(2,1)} %all-to-all-done.args_0_, bf16[8,8,32,128]{3,2,1,0:T(8,128)(2,1)} %bitcast.18, bf16[384,512]{1,0:T(8,128)(2,1)} %bitcast.16, bf16[128,256]{1,0:T(8,128)(2,1)} %constant.37.clone.args_3_.args_4_), custom_call_target="tpu_custom_call" | custom-call | tf_op jit(solution)/shard_map/score/pallas_call | solution.py:156
  113.1 0.9 select_add_fusion
  114.0 1.1 broadcast_in_dim.47
  115.1 8.7 %all-to-all-start.1 = ((f32[16,16,8,128]{3,2,1,0:T(8,128)}), f32[16,16,8,128]{3,2,1,0:T(8,128)S(1)}, u32[]{:S(2)}, u32[]{:S(2)}) async-start(f32[16,16,8,128]{3,2,1,0:T(8,128)} %broadcast_in_dim.47), calls=%async_computation.1 | async-start | bytes 2097152 | tf_op jit(solution)/shard_map/all_to_all | solution.py:316
  123.8 0.7 pad.9.args_3_
  124.5 14.0 %all-to-all-done.1.args_1_ = f32[16,16,8,128]{3,2,1,0:T(8,128)S(1)} async-done(((f32[16,16,8,128]{3,2,1,0:T(8,128)}), f32[16,16,8,128]{3,2,1,0:T(8,128)S(1)}, u32[]{:S(2)}, u32[]{:S(2)}) %all-to-all-start.1) | async-done | bytes 1048608 | tf_op jit(solution)/shard_map/all_to_all | solution.py:316
  138.5 1.0 copy-done
  139.5 39.4 %sums.1 = (f32[16,8,128]{2,1,0:T(8,128)}, bf16[8,9,32,128]{3,2,1,0:T(8,128)(2,1)}) custom-call(bf16[16,1056,128]{2,1,0:T(8,128)(2,1)} %all-to-all-done.args_0_, f32[16,16,8,128]{3,2,1,0:T(8,128)} %copy-done, bf16[384,512]{1,0:T(8,128)(2,1)} %bitcast.17, bf16[384,128]{1,0:T(8,128)(2,1)} %pad.9.args_3_, bf16[128,256]{1,0:T(8,128)(2,1)} %constant.37.clone.args_3_.args_4_), custom_call_target="tpu_custom_call" | custom-call | tf_op jit(solution)/shard_map/sums/pallas_call | solution.py:232
  178.9 7.6 %all-to-all-start.2 = ((bf16[8,9,32,128]{3,2,1,0:T(8,128)(2,1)}), bf16[8,9,32,128]{3,2,1,0:T(8,128)(2,1)S(1)}, u32[]{:S(2)}, u32[]{:S(2)}) async-start(bf16[8,9,32,128]{3,2,1,0:T(8,128)(2,1)} %get-tuple-element.4), calls=%async_computation.2 | async-start | bytes 1179648 | tf_op jit(solution)/shard_map/all_to_all | solution.py:319
  186.5 1.3 dynamic-slice_bitcast_fusion
  187.8 8.9 %all-to-all-done.2.args_0_ = bf16[8,9,32,128]{3,2,1,0:T(8,128)(2,1)S(1)} async-done(((bf16[8,9,32,128]{3,2,1,0:T(8,128)(2,1)}), bf16[8,9,32,128]{3,2,1,0:T(8,128)(2,1)S(1)}, u32[]{:S(2)}, u32[]{:S(2)}) %all-to-all-start.2) | async-done | bytes 589856 | tf_op jit(solution)/shard_map/all_to_all | solution.py:319
  196.7 0.8 copy-done.1
  197.5 1.9 finish.1
  (13 shorter events, 0.3 us)
Async XLA Ops:
  11.9 8.8 %copy-start.2 = (bf16[25,2,4,128]{3,2,1,0:T(4,128)(2,1)S(1)}, bf16[25,2,4,128]{3,2,1,0:T(4,128)(2,1)}, u32[]{:S(2)}) copy-start(bf16[25,2,4,128]{3,2,1,0:T(4,128)(2,1)} %param.9) | copy-start | bytes 153604
  11.9 74.3 %all-to-all-start = ((bf16[16,1056,128]{2,1,0:T(8,128)(2,1)}), bf16[16,1056,128]{2,1,0:T(8,128)(2,1)}, u32[]{:S(2)}, u32[]{:S(2)}) async-start(bf16[16,1056,128]{2,1,0:T(8,128)(2,1)} %cut.1), calls=%async_computation | async-start | bytes 8650752 | tf_op jit(solution)/shard_map/all_to_all | solution.py:302
  20.7 92.4 %copy-start.3 = (f32[128,8]{0,1:T(8,128)S(1)}, f32[128,8]{0,1:T(8,128)}, u32[]{:S(2)}) copy-start(f32[128,8]{0,1:T(8,128)} %param.13) | copy-start | bytes 12292
  115.1 23.4 %all-to-all-start.1 = ((f32[16,16,8,128]{3,2,1,0:T(8,128)}), f32[16,16,8,128]{3,2,1,0:T(8,128)S(1)}, u32[]{:S(2)}, u32[]{:S(2)}) async-start(f32[16,16,8,128]{3,2,1,0:T(8,128)} %broadcast_in_dim.47), calls=%async_computation.1 | async-start | bytes 2097152 | tf_op jit(solution)/shard_map/all_to_all | solution.py:316
  138.5 1.0 copy-start
  178.9 17.8 %all-to-all-start.2 = ((bf16[8,9,32,128]{3,2,1,0:T(8,128)(2,1)}), bf16[8,9,32,128]{3,2,1,0:T(8,128)(2,1)S(1)}, u32[]{:S(2)}, u32[]{:S(2)}) async-start(bf16[8,9,32,128]{3,2,1,0:T(8,128)(2,1)} %get-tuple-element.4), calls=%async_computation.2 | async-start | bytes 1179648 | tf_op jit(solution)/shard_map/all_to_all | solution.py:319
  196.7 0.8 copy-start.1

commit v2 on v1

v2 whole, which is shorter than its diff:
```python
import math

import jax
import jax.numpy as jnp
import numpy as np
from jax import lax
from jax.experimental import pallas as pl
from jax.experimental.pallas import tpu as pltpu
from jax.sharding import PartitionSpec as P

NROT = 36
SCORE_SCALE = 0.0025
REGULARIZER = 1.0

F32 = jnp.float32
BF16 = jnp.bfloat16
LANES = 128
INDEX_ROWS = 32
VMEM_LIMIT = 56 * 1024 * 1024


def split3_np(x):
    hi = x.astype(jnp.bfloat16)
    rest = x - hi.astype(np.float32)
    mid = rest.astype(jnp.bfloat16)
    low = (rest - mid.astype(np.float32)).astype(jnp.bfloat16)
    return hi, mid, low


def rounded(x):
    return lax.reduce_precision(x, exponent_bits=8, mantissa_bits=7)


def split3(x):
    hi = rounded(x)
    rest = x - hi
    mid = rounded(rest)
    low = rounded(rest - mid)
    return hi.astype(BF16), mid.astype(BF16), low.astype(BF16)


def phase_table(harmonics):
    turns = (np.arange(NROT)[:, None] * np.arange(harmonics)[None, :]) % NROT
    angle = turns.astype(np.float32) * np.float32(2.0 * math.pi / NROT)
    both = np.concatenate([np.cos(angle), np.sin(angle)], axis=1).astype(np.float32)
    stacked = np.concatenate(split3_np(both), axis=0)
    pad = np.zeros((128 - 3 * NROT, 2 * harmonics), stacked.dtype)
    return np.concatenate([stacked, pad], axis=0).T


def cut_kernel(share, x_ref, index_ref, out_ref):
    step = pl.program_id(0)
    block, parts, cycles, lanes = x_ref.shape
    owners = out_ref.shape[0]
    for part in range(parts):
        for first in range(0, cycles, 8):
            swapped = jnp.swapaxes(x_ref[:, part, first : first + 8, :], 0, 1)
            for i in range(8):
                owner, slab = (first + i) // share, part * share + (first + i) % share
                out_ref[owner, pl.ds(pl.multiple_of(slab * 128 + step * block, block), block), :] = swapped[i]

    @pl.when(step == 0)
    def _():
        for owner in range(owners):
            out_ref[owner, 2 * share * 128 :, :] = index_ref[...]


def cut_particles(particles, index_rows, owners):
    count, parts, cycles, lanes = particles.shape
    share = cycles // owners
    block = 32
    out_rows = 2 * share * count + INDEX_ROWS
    return pl.pallas_call(
        lambda *refs: cut_kernel(share, *refs),
        name="cut",
        grid=(count // block,),
        in_specs=[
            pl.BlockSpec((block, parts, cycles, lanes), lambda s: (s, 0, 0, 0)),
            pl.BlockSpec((INDEX_ROWS, lanes), lambda s: (0, 0)),
        ],
        out_specs=pl.BlockSpec((owners, out_rows, lanes), lambda s: (0, 0, 0)),
        out_shape=jax.ShapeDtypeStruct((owners, out_rows, lanes), BF16),
        compiler_params=pltpu.CompilerParams(vmem_limit_bytes=VMEM_LIMIT),
    )(particles, index_rows)


def row_iota(rows):
    return lax.broadcasted_iota(jnp.int32, (rows, LANES), 0)


def hot_rows(row, wanted):
    return jnp.where(row == wanted, 1.0, 0.0).astype(BF16)


def ctf_rows(index_rows, ctf_parts):
    groups = hot_rows(index_rows[16:17], row_iota(LANES).astype(F32))
    three = jnp.dot(ctf_parts[...], groups, preferred_element_type=F32)
    return three[0:8] + three[8:16] + three[16:24]


def rotations(index_rows, top, phases):
    rows = row_iota(LANES)
    within = jnp.where(rows < 3 * NROT, rows % NROT, -1).astype(F32)
    hot = jnp.concatenate([hot_rows(index_rows[8 + j : 9 + j], within) for j in range(top)], axis=1)
    return jnp.dot(phases[...], hot, preferred_element_type=F32)


def prepare(s, slot, slabs, top, x_ref, ctf_parts, phases, index, ctf, scaled, angles):
    index[slot][...] = x_ref[s, slabs * 128 :, :].astype(F32)
    rows = index[slot][...]
    ctf[slot][...] = ctf_rows(rows, ctf_parts)
    for slab in range(slabs):
        r = slab % (slabs // 2)
        scaled[slot][slab] = x_ref[s, slab * 128 : (slab + 1) * 128, :].T.astype(F32) * ctf[slot][r : r + 1, :]
    angles[slot][...] = rotations(rows, top, phases)


def prepared_scratch(slabs, top):
    return [
        [pltpu.VMEM((INDEX_ROWS, LANES), F32)] * 2,
        [pltpu.VMEM((8, LANES), F32)] * 2,
        [pltpu.VMEM((slabs, 128, LANES), F32)] * 2,
        [pltpu.VMEM((256, top * 128), F32)] * 2,
    ]


def score_kernel(slabs, top, x_ref, refs_ref, ctf_parts, phases, out_ref, table, picked, index, ctf, scaled, angles):
    half = slabs // 2

    @pl.when(pl.program_id(0) == 0)
    def _():
        for slab in range(slabs):
            for piece in range(2):
                devs = [refs_ref[piece * 4 + dev, slab] for dev in range(4)]
                table[slab * 128 : (slab + 1) * 128, piece * 128 : (piece + 1) * 128] = jnp.concatenate(devs, axis=0).T.astype(BF16)

    classes = row_iota(256).astype(F32)

    def gather(slot, pair):
        hot = jnp.concatenate([hot_rows(index[slot][j : j + 1, :], classes) for j in (2 * pair, 2 * pair + 1)], axis=1)
        picked[pair % 2][...] = jnp.dot(table[...], hot, preferred_element_type=F32)

    def consume(slot, pair, side):
        j = 2 * pair + side
        across = slice(j * 128, (j + 1) * 128)
        here = slice(side * 128, (side + 1) * 128)
        even = odd = None
        for r in range(half):
            ref_re = picked[pair % 2][r * 128 : (r + 1) * 128, here]
            ref_im = picked[pair % 2][(half + r) * 128 : (half + r + 1) * 128, here]
            re, im = scaled[slot][r], scaled[slot][half + r]
            a = re * ref_re + im * ref_im
            b = re * ref_im - im * ref_re
            even = a if even is None else even + a
            odd = b if odd is None else odd + b
        return jnp.sum(angles[slot][:128, across] * even + angles[slot][128:, across] * odd, axis=0, keepdims=True)

    for s in range(x_ref.shape[0]):
        slot = s % 2
        prepare(s, slot, slabs, top, x_ref, ctf_parts, phases, index, ctf, scaled, angles)
        scores = []
        for pair in range(top // 2):
            gather(slot, pair)
            scores += [consume(slot, pair, 0), consume(slot, pair, 1)]
        out_ref[s] = SCORE_SCALE * jnp.concatenate(scores, axis=0)


def partial_scores(moved, refs, ctf_parts, phases, slabs, top):
    sources, rows, lanes = moved.shape
    whole = lambda a: pl.BlockSpec(a.shape, lambda s, n=a.ndim: (0,) * n)
    return pl.pallas_call(
        lambda *args: score_kernel(slabs, top, *args),
        name="score",
        grid=(sources // 2,),
        in_specs=[pl.BlockSpec((2, rows, lanes), lambda s: (s, 0, 0)), whole(refs), whole(ctf_parts), whole(phases)],
        out_specs=pl.BlockSpec((2, top, lanes), lambda s: (s, 0, 0)),
        out_shape=jax.ShapeDtypeStruct((sources, top, lanes), F32),
        scratch_shapes=[pltpu.VMEM((slabs * 128, 256), BF16), [pltpu.VMEM((slabs * 128, 256), F32)] * 2]
        + prepared_scratch(slabs, top),
        compiler_params=pltpu.CompilerParams(vmem_limit_bytes=VMEM_LIMIT),
    )(moved, refs, ctf_parts, phases)


def parted(x):
    hi = x.astype(BF16).astype(F32)
    rest = x - hi
    mid = rest.astype(BF16).astype(F32)
    return jnp.concatenate([hi, mid, rest - mid, jnp.zeros_like(x)], axis=0)


def sum_kernel(
    slabs, top, x_ref, partial_ref, ctf_parts, phases, weight_ref, out_ref, contribution, hots, total, index, ctf, scaled, angles
):
    half = slabs // 2
    sources = x_ref.shape[0]
    score = partial_ref[0]
    for source in range(1, sources):
        score = score + partial_ref[source]
    raised = jnp.exp(score - jnp.max(score, axis=1, keepdims=True))
    weight_ref[...] = raised / jnp.sum(raised, axis=1, keepdims=True)
    total[...] = jnp.zeros_like(total)
    contribution[1][...] = jnp.zeros_like(contribution[1][...])
    hots[1][...] = jnp.zeros_like(hots[1][...])
    classes = row_iota(256).astype(F32)

    def contribute(s, slot, j):
        across = slice(j * 128, (j + 1) * 128)
        w = weight_ref[s, j : j + 1, :]
        wc = w * angles[slot][:128, across]
        ws = w * angles[slot][128:, across]
        for r in range(half):
            re, im = scaled[slot][r], scaled[slot][half + r]
            contribution[slot][r * 128 : (r + 1) * 128, across] = (re * wc - im * ws).astype(BF16)
            contribution[slot][(half + r) * 128 : (half + r + 1) * 128, across] = (re * ws + im * wc).astype(BF16)
        contribution[slot][slabs * 128 :, across] = parted(w * (ctf[slot][...] * ctf[slot][...])).astype(BF16)
        hots[slot][:, across] = hot_rows(index[slot][j : j + 1, :], classes)

    def accumulate(slot):
        total[...] += lax.dot_general(
            contribution[slot][...], hots[slot][...], (((1,), (1,)), ((), ())), preferred_element_type=F32
        )

    def advance(s, slot):
        prepare(s, slot, slabs, top, x_ref, ctf_parts, phases, index, ctf, scaled, angles)
        accumulate(1 - slot)
        for j in range(top):
            contribute(s, slot, j)

    @pl.loop(0, sources // 2)
    def _(i):
        advance(2 * i, 0)
        advance(2 * i + 1, 1)

    accumulate(1)
    n = total[slabs * 128 :, :]
    coded = parted(n[0:8] + n[8:16] + n[16:24])
    coded = jnp.concatenate([coded, jnp.zeros((LANES - INDEX_ROWS, 256), F32)], axis=0)
    for slab in range(slabs + 1):
        piece = (total[slab * 128 : (slab + 1) * 128, :] if slab < slabs else coded).T.astype(BF16)
        for dev in range(out_ref.shape[0]):
            out_ref[dev, slab] = piece[dev * 32 : (dev + 1) * 32]


def weighted_sums(moved, partials, ctf_parts, phases, slabs, top, owners):
    sources, rows, lanes = moved.shape
    return pl.pallas_call(
        lambda *args: sum_kernel(slabs, top, *args),
        name="sums",
        out_shape=[
            jax.ShapeDtypeStruct((sources, top, lanes), F32),
            jax.ShapeDtypeStruct((owners, slabs + 1, 32, lanes), BF16),
        ],
        scratch_shapes=[
            [pltpu.VMEM((rows, top * 128), BF16)] * 2,
            [pltpu.VMEM((256, top * 128), BF16)] * 2,
            pltpu.VMEM((rows, 256), F32),
        ]
        + prepared_scratch(slabs, top),
        compiler_params=pltpu.CompilerParams(vmem_limit_bytes=VMEM_LIMIT),
    )(moved, partials, ctf_parts, phases)


def finish_kernel(slabs, owned, parts_ref, out_ref):
    half = slabs // 2

    def gathered(slab):
        value = parts_ref[0, slab].astype(F32)
        for source in range(1, parts_ref.shape[0]):
            value = value + parts_ref[source, slab].astype(F32)
        return value

    coded = gathered(slabs)
    norm = coded + pltpu.roll(coded, LANES - 8, 1) + pltpu.roll(coded, LANES - 16, 1) + REGULARIZER
    for r in range(half):
        scale = 1.0 / norm[:, r : r + 1]
        for part in range(2):
            out_ref[:, part, r, :] = (gathered(part * half + r) * scale)[:owned]


def finish(parts, owned, slabs):
    return pl.pallas_call(
        lambda *args: finish_kernel(slabs, owned, *args),
        name="finish",
        out_shape=jax.ShapeDtypeStruct((owned, 2, slabs // 2, LANES), F32),
        compiler_params=pltpu.CompilerParams(vmem_limit_bytes=VMEM_LIMIT),
    )(parts)


def body(particles, references, class_index, rotation_index, defocus_group, log_prior, ctf_table):
    count, _, cycles, harmonics = particles.shape
    owned, _, share, _ = references.shape
    top = class_index.shape[1]
    owners = cycles // share
    slabs = 2 * share
    me = lax.axis_index("dp")

    padded = class_index + (32 - owned) * (class_index // owned)
    index_rows = jnp.concatenate(
        [padded, rotation_index, defocus_group[:, None], jnp.zeros((count, INDEX_ROWS - 2 * top - 1), jnp.int32)], axis=1
    )
    index_rows = index_rows.T.astype(BF16)
    send = cut_particles(particles, index_rows, owners)
    moved = lax.all_to_all(send, "dp", 0, 0)

    own_refs = jnp.pad(references.transpose(1, 2, 0, 3).reshape(slabs, owned, harmonics), ((0, 0), (0, 32 - owned), (0, 0)))
    refs = lax.all_gather(own_refs.astype(F32), "cls", axis=0)

    ctf = lax.dynamic_slice(ctf_table, (0, me * share), (ctf_table.shape[0], share)).T
    ctf = jnp.pad(ctf, ((0, 8 - share), (0, 0)))
    ctf_parts = jnp.concatenate(split3(ctf), axis=0)
    phases = jnp.asarray(phase_table(harmonics))

    partial = partial_scores(moved, refs, ctf_parts, phases, slabs, top)
    mine = (jnp.arange(owners) == me)[:, None, None]
    partial = partial + jnp.where(mine, log_prior.T[None], 0.0)
    partials = lax.all_to_all(jnp.broadcast_to(partial[None], (owners,) + partial.shape), "dp", 0, 0)

    weights, sums = weighted_sums(moved, partials, ctf_parts, phases, slabs, top, refs.shape[0])
    parts = lax.all_to_all(sums, "cls", 0, 0)
    new_references = finish(parts, owned, slabs)
    own_weights = lax.dynamic_index_in_dim(weights, me, 0, keepdims=False).T
    return new_references, own_weights


def solution(mesh):
    in_specs = (
        P(("dp", "cls"), None, None, None),
        P("cls", None, "dp", None),
        P(("dp", "cls"), None),
        P(("dp", "cls"), None),
        P(("dp", "cls")),
        P(("dp", "cls"), None),
        P(),
    )
    out_specs = (P("cls", None, "dp", None), P(("dp", "cls"), None))
    return jax.shard_map(body, mesh=mesh, in_specs=in_specs, out_specs=out_specs, check_vma=False)
```

time: 200 us -> 190 us (0.950)
  Pallas kernels: 76.7 us -> 55.5 us
  between operations: 0.72 us -> 14.1 us
  starting transfers between devices: 25.1 us -> 16.4 us
  blocking collectives: 15.3 us -> 23.3 us
  local copies, waits for them, and re-layouts: 6.37 us -> 2.32 us
  waiting for transfers between devices: 70.9 us -> 73 us
    all_gather x0 -> x1, waiting for transfers between devices: none -> 26.7 us  [body(): refs = lax.all_gather(own_refs.astype(F32), 'cls', axis=0)]
    all_to_all x0 -> x1, blocking collectives: none -> 23.3 us  [body(): lax.all_to_all(jnp.broadcast_to(partial[None], (owners,) + partial.shape)...]
    all_gather x1 -> x0, blocking collectives: 15.3 us -> none  [body(): refs = lax.all_gather(own_refs, 'cls', axis=0)]
    all_to_all x1 -> x0, waiting for transfers between devices: 14 us -> none  [body(): lax.all_to_all(jnp.broadcast_to(partial[None], (owners,) + partial.shape)...]
    pallas_call x1, Pallas kernels: 39.4 us -> 25.8 us  [weighted_sums(): pl.pallas_call(lambda *args: sum_kernel(slabs, top, *args), name='sums',...]
    all_to_all x1, waiting for transfers between devices: 48 us -> 37.4 us  [body(): moved = lax.all_to_all(send, 'dp', 0, 0)]
    all_to_all x1 -> x0, starting transfers between devices: 8.71 us -> none  [body(): lax.all_to_all(jnp.broadcast_to(partial[None], (owners,) + partial.shape)...]
    pallas_call x1, Pallas kernels: 26.9 us -> 22.1 us  [partial_scores(): pl.pallas_call(lambda *args: score_kernel(slabs, top, *args), name='score...]
  transfers between devices with their start and end apart: 3 -> 3, of which waited for: 3 -> 3; matrix products, arithmetic and copies ran while one was open for 2% -> 1% of each run, Pallas kernels for 0% -> 0%
where the time goes in v2:
time: 190 us
  waiting for transfers between devices  73 us (38%)
  Pallas kernels  55.5 us (29%)
  blocking collectives  23.3 us (12%)
  starting transfers between devices  16.4 us (9%)
  between operations  14.1 us (7%)
  other arithmetic  4.92 us (3%)
  local copies, waits for them, and re-layouts  2.32 us (1%)
    all_to_all x1, waiting for transfers between devices, body(): moved = lax.all_to_all(send, 'dp', 0, 0)  37.4 us
    all_gather x1, waiting for transfers between devices, body(): refs = lax.all_gather(own_refs.astype(F32), 'cls', axis=0)  26.7 us
    pallas_call x1, Pallas kernels, weighted_sums(): pl.pallas_call(lambda *args: sum_kernel(slabs, top, *args), name='sums',...  25.8 us
    all_to_all x1, blocking collectives, body(): lax.all_to_all(jnp.broadcast_to(partial[None], (owners,) + partial.shape)...  23.3 us
    pallas_call x1, Pallas kernels, partial_scores(): pl.pallas_call(lambda *args: score_kernel(slabs, top, *args), name='score...  22.1 us
    all_to_all x1, waiting for transfers between devices, body(): parts = lax.all_to_all(sums, 'cls', 0, 0)  8.9 us
    all_to_all x1, starting transfers between devices, body(): moved = lax.all_to_all(send, 'dp', 0, 0)  8.77 us
    all_to_all x1, starting transfers between devices, body(): parts = lax.all_to_all(sums, 'cls', 0, 0)  7.61 us
  transfers between devices with their start and end apart: 3, of which 3 were waited for; matrix products, arithmetic and copies ran while one was open for 1% of the time, Pallas kernels for 0%

profile of v2, /device:TPU:1, one launch (start us, length us, event | category | flops | bytes accessed | tf_op | source)
XLA Modules:
  0.0 189.6 jit_solution(15631059662159042250)
XLA Ops:
  7.2 0.0 copy-start
  7.2 0.7 convert_bitcast_fusion
  7.8 0.7 convert.14
  8.5 0.7 fusion.4
  9.2 0.1 pad.16.clone
  9.3 0.7 maximum_bitcast_fusion.refs_1_
  10.0 5.6 %cut.1 = bf16[16,1056,128]{2,1,0:T(8,128)(2,1)} custom-call(bf16[128,2,64,128]{3,2,1,0:T(8,128)(2,1)} %refs_0_.1, bf16[32,128]{1,0:T(8,128)(2,1)} %maximum_bitcast_fusion.refs_1_), custom_call_target="tpu_custom_call" | custom-call | tf_op jit(solution)/shard_map/cut/pallas_call | solution.py:73
  15.6 8.8 %all-to-all-start = ((bf16[16,1056,128]{2,1,0:T(8,128)(2,1)}), bf16[16,1056,128]{2,1,0:T(8,128)(2,1)}, u32[]{:S(2)}, u32[]{:S(2)}) async-start(bf16[16,1056,128]{2,1,0:T(8,128)(2,1)} %cut.1), calls=%async_computation | async-start | bytes 8650752 | tf_op jit(solution)/shard_map/all_to_all | solution.py:303
  24.4 0.0 all-gather.3.cloned.1.call-start
  24.5 0.7 pad_convert_fusion
  25.2 0.0 all-gather.3.cloned.1.call-update
  25.3 0.6 pad_maximum_fusion.args_2_
  25.9 26.7 %all-gather.3.cloned.1.call-done = f32[64,32,128]{2,1,0:T(8,128)} async-done(((f32[8,32,128]{2,1,0:T(8,128)}), f32[64,32,128]{2,1,0:T(8,128)}) %all-gather.3.cloned.1.call-update) | async-done | bytes 1048592 | tf_op jit(solution)/shard_map/all_gather | solution.py:306
  52.6 37.4 %all-to-all-done.args_0_ = bf16[16,1056,128]{2,1,0:T(8,128)(2,1)} async-done(((bf16[16,1056,128]{2,1,0:T(8,128)(2,1)}), bf16[16,1056,128]{2,1,0:T(8,128)(2,1)}, u32[]{:S(2)}, u32[]{:S(2)}) %all-to-all-start) | async-done | bytes 4325408 | tf_op jit(solution)/shard_map/all_to_all | solution.py:303
  90.0 22.1 %score.1 = f32[16,8,128]{2,1,0:T(8,128)} custom-call(bf16[16,1056,128]{2,1,0:T(8,128)(2,1)} %all-to-all-done.args_0_, f32[8,8,32,128]{3,2,1,0:T(8,128)} %bitcast.14, bf16[24,128]{1,0:T(8,128)(2,1)} %pad_maximum_fusion.args_2_, bf16[256,128]{1,0:T(8,128)(2,1)} %constant.38.clone.args_3_), custom_call_target="tpu_custom_call" | custom-call | tf_op jit(solution)/shard_map/score/pallas_call | solution.py:171
  112.1 0.9 select_add_fusion
  113.1 0.1 broadcast_in_dim.40
  113.2 23.3 %all_to_all.15.args_1_ = f32[16,16,8,128]{3,2,1,0:T(8,128)} all-to-all(f32[16,16,8,128]{3,2,1,0:T(8,128)S(1)} %broadcast_in_dim.40), channel_id=1, replica_groups=mesh['dp'=16,'cls'=8] {'dp'}, dimensions={0} | all-to-all | bytes 2097152 | tf_op jit(solution)/shard_map/all_to_all | solution.py:316
  136.4 25.8 %sums.1 = (f32[16,8,128]{2,1,0:T(8,128)}, bf16[8,9,32,128]{3,2,1,0:T(8,128)(2,1)}) custom-call(bf16[16,1056,128]{2,1,0:T(8,128)(2,1)} %all-to-all-done.args_0_, f32[16,16,8,128]{3,2,1,0:T(8,128)} %all_to_all.15.args_1_, bf16[24,128]{1,0:T(8,128)(2,1)} %pad_maximum_fusion.args_2_, bf16[256,128]{1,0:T(8,128)(2,1)} %constant.38.clone.args_3_), custom_call_target="tpu_custom_call" | custom-call | tf_op jit(solution)/shard_map/sums/pallas_call | solution.py:246
  162.2 7.6 %all-to-all-start.2 = ((bf16[8,9,32,128]{3,2,1,0:T(8,128)(2,1)}), bf16[8,9,32,128]{3,2,1,0:T(8,128)(2,1)S(1)}, u32[]{:S(2)}, u32[]{:S(2)}) async-start(bf16[8,9,32,128]{3,2,1,0:T(8,128)(2,1)} %get-tuple-element.4), calls=%async_computation.2 | async-start | bytes 1179648 | tf_op jit(solution)/shard_map/all_to_all | solution.py:319
  169.8 1.3 dynamic-slice_bitcast_fusion
  171.1 8.9 %all-to-all-done.2.args_0_ = bf16[8,9,32,128]{3,2,1,0:T(8,128)(2,1)S(1)} async-done(((bf16[8,9,32,128]{3,2,1,0:T(8,128)(2,1)}), bf16[8,9,32,128]{3,2,1,0:T(8,128)(2,1)S(1)}, u32[]{:S(2)}, u32[]{:S(2)}) %all-to-all-start.2) | async-done | bytes 589856 | tf_op jit(solution)/shard_map/all_to_all | solution.py:319
  180.0 0.8 copy-done.1
  180.8 1.9 %finish.1 = f32[25,2,4,128]{3,2,1,0:T(4,128)} custom-call(bf16[8,9,32,128]{3,2,1,0:T(8,128)(2,1)} %copy-done.1), custom_call_target="tpu_custom_call" | custom-call | tf_op jit(solution)/shard_map/finish/pallas_call | solution.py:281
  (11 shorter events, 0.1 us)
Async XLA Ops:
  7.2 18.1 %copy-start = (f32[128,64]{0,1:T(8,128)S(1)}, f32[128,64]{0,1:T(8,128)}, u32[]{:S(2)}) copy-start(f32[128,64]{0,1:T(8,128)} %param.14) | copy-start | bytes 98308
  15.6 8.8 %copy-start.2 = (bf16[25,2,4,128]{3,2,1,0:T(4,128)(2,1)S(1)}, bf16[25,2,4,128]{3,2,1,0:T(4,128)(2,1)}, u32[]{:S(2)}) copy-start(bf16[25,2,4,128]{3,2,1,0:T(4,128)(2,1)} %param.9) | copy-start | bytes 153604
  15.6 74.3 %all-to-all-start = ((bf16[16,1056,128]{2,1,0:T(8,128)(2,1)}), bf16[16,1056,128]{2,1,0:T(8,128)(2,1)}, u32[]{:S(2)}, u32[]{:S(2)}) async-start(bf16[16,1056,128]{2,1,0:T(8,128)(2,1)} %cut.1), calls=%async_computation | async-start | bytes 8650752 | tf_op jit(solution)/shard_map/all_to_all | solution.py:303
  24.4 87.7 %copy-start.3 = (f32[128,8]{0,1:T(8,128)S(1)}, f32[128,8]{0,1:T(8,128)}, u32[]{:S(2)}) copy-start(f32[128,8]{0,1:T(8,128)} %param.13) | copy-start | bytes 12292
  24.4 28.1 %all-gather.3.cloned.1.call-start = ((), (), s32[]{:S(2)}) async-start(), calls=%async_computation.3 | async-start | bytes 1179648 | tf_op jit(solution)/shard_map/all_gather | solution.py:306
  162.2 17.8 %all-to-all-start.2 = ((bf16[8,9,32,128]{3,2,1,0:T(8,128)(2,1)}), bf16[8,9,32,128]{3,2,1,0:T(8,128)(2,1)S(1)}, u32[]{:S(2)}, u32[]{:S(2)}) async-start(bf16[8,9,32,128]{3,2,1,0:T(8,128)(2,1)} %get-tuple-element.4), calls=%async_computation.2 | async-start | bytes 1179648 | tf_op jit(solution)/shard_map/all_to_all | solution.py:319
  180.0 0.8 copy-start.1
Sparse Core Ops, SparseCore 0:
  27.0 25.5 all-gather.2

commit v3 on v2

v3 whole, which is shorter than its diff:
```python
import math

import jax
import jax.numpy as jnp
import numpy as np
from jax import lax
from jax.experimental import pallas as pl
from jax.experimental.pallas import tpu as pltpu
from jax.sharding import PartitionSpec as P

NROT = 36
SCORE_SCALE = 0.0025
REGULARIZER = 1.0

F32 = jnp.float32
BF16 = jnp.bfloat16
LANES = 128
INDEX_ROWS = 32
VMEM_LIMIT = 56 * 1024 * 1024


def split3_np(x):
    hi = x.astype(jnp.bfloat16)
    rest = x - hi.astype(np.float32)
    mid = rest.astype(jnp.bfloat16)
    low = (rest - mid.astype(np.float32)).astype(jnp.bfloat16)
    return hi, mid, low


def rounded(x):
    return lax.reduce_precision(x, exponent_bits=8, mantissa_bits=7)


def split3(x):
    hi = rounded(x)
    rest = x - hi
    mid = rounded(rest)
    low = rounded(rest - mid)
    return hi.astype(BF16), mid.astype(BF16), low.astype(BF16)


def phase_table(harmonics):
    turns = (np.arange(NROT)[:, None] * np.arange(harmonics)[None, :]) % NROT
    angle = turns.astype(np.float32) * np.float32(2.0 * math.pi / NROT)
    both = np.concatenate([np.cos(angle), np.sin(angle)], axis=1).astype(np.float32)
    stacked = np.concatenate(split3_np(both), axis=0)
    pad = np.zeros((128 - 3 * NROT, 2 * harmonics), stacked.dtype)
    return np.concatenate([stacked, pad], axis=0).T


def cut_kernel(share, x_ref, index_ref, out_ref):
    step = pl.program_id(0)
    block, parts, cycles, lanes = x_ref.shape
    owners = out_ref.shape[0]
    for part in range(parts):
        for first in range(0, cycles, 8):
            swapped = jnp.swapaxes(x_ref[:, part, first : first + 8, :], 0, 1)
            for i in range(8):
                owner, slab = (first + i) // share, part * share + (first + i) % share
                out_ref[owner, pl.ds(pl.multiple_of(slab * 128 + step * block, block), block), :] = swapped[i]

    @pl.when(step == 0)
    def _():
        for owner in range(owners):
            out_ref[owner, 2 * share * 128 :, :] = index_ref[...]


def cut_particles(particles, index_rows, owners):
    count, parts, cycles, lanes = particles.shape
    share = cycles // owners
    block = 32
    out_rows = 2 * share * count + INDEX_ROWS
    return pl.pallas_call(
        lambda *refs: cut_kernel(share, *refs),
        name="cut",
        grid=(count // block,),
        in_specs=[
            pl.BlockSpec((block, parts, cycles, lanes), lambda s: (s, 0, 0, 0)),
            pl.BlockSpec((INDEX_ROWS, lanes), lambda s: (0, 0)),
        ],
        out_specs=pl.BlockSpec((owners, out_rows, lanes), lambda s: (0, 0, 0)),
        out_shape=jax.ShapeDtypeStruct((owners, out_rows, lanes), BF16),
        compiler_params=pltpu.CompilerParams(vmem_limit_bytes=VMEM_LIMIT),
    )(particles, index_rows)


def row_iota(rows):
    return lax.broadcasted_iota(jnp.int32, (rows, LANES), 0)


def hot_rows(row, wanted):
    return jnp.where(row == wanted, 1.0, 0.0).astype(BF16)


def ctf_rows(index_rows, ctf_parts):
    groups = hot_rows(index_rows[16:17], row_iota(LANES).astype(F32))
    three = jnp.dot(ctf_parts[...], groups, preferred_element_type=F32)
    return three[0:8] + three[8:16] + three[16:24]


def rotations(index_rows, top, phases):
    rows = row_iota(LANES)
    within = jnp.where(rows < 3 * NROT, rows % NROT, -1).astype(F32)
    hot = jnp.concatenate([hot_rows(index_rows[8 + j : 9 + j], within) for j in range(top)], axis=1)
    return jnp.dot(phases[...], hot, preferred_element_type=F32)


def prepared(s, slabs, top, x_ref, ctf_parts, phases):
    rows = x_ref[s, slabs * 128 :, :].astype(F32)
    ctf = ctf_rows(rows, ctf_parts)
    scaled = []
    for slab in range(slabs):
        r = slab % (slabs // 2)
        scaled.append(x_ref[s, slab * 128 : (slab + 1) * 128, :].T.astype(F32) * ctf[r : r + 1, :])
    return rows, ctf, scaled, rotations(rows, top, phases)


def score_kernel(slabs, top, x_ref, refs_ref, ctf_parts, phases, prior_ref, out_ref, table):
    half = slabs // 2

    @pl.when(pl.program_id(0) == 0)
    def _():
        for slab in range(slabs):
            for piece in range(2):
                devs = [refs_ref[piece * 4 + dev, slab].astype(F32) for dev in range(4)]
                table[slab * 128 : (slab + 1) * 128, piece * 128 : (piece + 1) * 128] = jnp.concatenate(devs, axis=0).T.astype(BF16)

    classes = row_iota(256).astype(F32)

    for s in range(x_ref.shape[0]):
        index, _, scaled, angles = prepared(s, slabs, top, x_ref, ctf_parts, phases)
        scores = []
        for pair in range(top // 2):
            hot = jnp.concatenate([hot_rows(index[j : j + 1, :], classes) for j in (2 * pair, 2 * pair + 1)], axis=1)
            picked = jnp.dot(table[...], hot, preferred_element_type=F32)
            for side in range(2):
                across = slice((2 * pair + side) * 128, (2 * pair + side + 1) * 128)
                here = slice(side * 128, (side + 1) * 128)
                even = odd = None
                for r in range(half):
                    ref_re = picked[r * 128 : (r + 1) * 128, here]
                    ref_im = picked[(half + r) * 128 : (half + r + 1) * 128, here]
                    re, im = scaled[r], scaled[half + r]
                    a = re * ref_re + im * ref_im
                    b = re * ref_im - im * ref_re
                    even = a if even is None else even + a
                    odd = b if odd is None else odd + b
                scores.append(jnp.sum(angles[:128, across] * even + angles[128:, across] * odd, axis=0, keepdims=True))
        out_ref[s] = SCORE_SCALE * jnp.concatenate(scores, axis=0) + prior_ref[s]


def partial_scores(moved, refs, ctf_parts, phases, prior, slabs, top):
    sources, rows, lanes = moved.shape
    whole = lambda a: pl.BlockSpec(a.shape, lambda s, n=a.ndim: (0,) * n)
    return pl.pallas_call(
        lambda *args: score_kernel(slabs, top, *args),
        name="score",
        grid=(sources // 2,),
        in_specs=[
            pl.BlockSpec((2, rows, lanes), lambda s: (s, 0, 0)),
            whole(refs),
            whole(ctf_parts),
            whole(phases),
            pl.BlockSpec((2, top, lanes), lambda s: (s, 0, 0)),
        ],
        out_specs=pl.BlockSpec((2, top, lanes), lambda s: (s, 0, 0)),
        out_shape=jax.ShapeDtypeStruct((sources, top, lanes), F32),
        scratch_shapes=[pltpu.VMEM((slabs * 128, 256), BF16)],
        compiler_params=pltpu.CompilerParams(vmem_limit_bytes=VMEM_LIMIT),
    )(moved, refs, ctf_parts, phases, prior)


def parted(x):
    hi = x.astype(BF16).astype(F32)
    rest = x - hi
    mid = rest.astype(BF16).astype(F32)
    return jnp.concatenate([hi, mid, rest - mid, jnp.zeros_like(x)], axis=0)


def sum_kernel(slabs, top, x_ref, partial_ref, ctf_parts, phases, weight_ref, out_ref, total):
    half = slabs // 2
    step = pl.program_id(0)

    @pl.when(step == 0)
    def _():
        total[...] = jnp.zeros_like(total)

    classes = row_iota(256).astype(F32)
    score = partial_ref[0]
    for source in range(1, partial_ref.shape[0]):
        score = score + partial_ref[source]
    raised = jnp.exp(score - jnp.max(score, axis=1, keepdims=True))
    weights = raised / jnp.sum(raised, axis=1, keepdims=True)
    parts, hots = [], []
    for s in range(x_ref.shape[0]):
        index, ctf, scaled, angles = prepared(s, slabs, top, x_ref, ctf_parts, phases)
        squared = ctf * ctf
        weight = weights[s]
        for pair in range(top // 2):
            for j in (2 * pair, 2 * pair + 1):
                across = slice(j * 128, (j + 1) * 128)
                w = weight[j : j + 1, :]
                wc = w * angles[:128, across]
                ws = w * angles[128:, across]
                column = [(scaled[r] * wc - scaled[half + r] * ws).astype(BF16) for r in range(half)]
                column += [(scaled[r] * ws + scaled[half + r] * wc).astype(BF16) for r in range(half)]
                column.append(parted(w * squared).astype(BF16))
                parts.append(jnp.concatenate(column, axis=0))
                hots.append(hot_rows(index[j : j + 1, :], classes))
    total[...] += lax.dot_general(
        jnp.concatenate(parts, axis=1), jnp.concatenate(hots, axis=1), (((1,), (1,)), ((), ())), preferred_element_type=F32
    )
    weight_ref[...] = weights

    @pl.when(step == pl.num_programs(0) - 1)
    def _():
        n = total[slabs * 128 :, :]
        coded = parted(n[0:8] + n[8:16] + n[16:24])
        coded = jnp.concatenate([coded, jnp.zeros((LANES - INDEX_ROWS, 256), F32)], axis=0)
        for slab in range(slabs + 1):
            piece = (total[slab * 128 : (slab + 1) * 128, :] if slab < slabs else coded).T.astype(BF16)
            for dev in range(out_ref.shape[0]):
                out_ref[dev, slab] = piece[dev * 32 : (dev + 1) * 32]


def weighted_sums(moved, partials, ctf_parts, phases, slabs, top, owners):
    sources, rows, lanes = moved.shape
    whole = lambda a: pl.BlockSpec(a.shape, lambda s, n=a.ndim: (0,) * n)
    out = (owners, slabs + 1, 32, lanes)
    return pl.pallas_call(
        lambda *args: sum_kernel(slabs, top, *args),
        name="sums",
        grid=(sources // 4,),
        in_specs=[
            pl.BlockSpec((4, rows, lanes), lambda s: (s, 0, 0)),
            pl.BlockSpec((sources, 4, top, lanes), lambda s: (0, s, 0, 0)),
            whole(ctf_parts),
            whole(phases),
        ],
        out_specs=[
            pl.BlockSpec((4, top, lanes), lambda s: (s, 0, 0)),
            pl.BlockSpec(out, lambda s: (0, 0, 0, 0)),
        ],
        out_shape=[jax.ShapeDtypeStruct((sources, top, lanes), F32), jax.ShapeDtypeStruct(out, BF16)],
        scratch_shapes=[pltpu.VMEM((rows, 256), F32)],
        compiler_params=pltpu.CompilerParams(vmem_limit_bytes=VMEM_LIMIT),
    )(moved, partials, ctf_parts, phases)


def finish_kernel(slabs, owned, parts_ref, out_ref):
    half = slabs // 2

    def gathered(slab):
        value = parts_ref[0, slab].astype(F32)
        for source in range(1, parts_ref.shape[0]):
            value = value + parts_ref[source, slab].astype(F32)
        return value

    coded = gathered(slabs)
    norm = coded + pltpu.roll(coded, LANES - 8, 1) + pltpu.roll(coded, LANES - 16, 1) + REGULARIZER
    for r in range(half):
        scale = 1.0 / norm[:, r : r + 1]
        for part in range(2):
            out_ref[:, part, r, :] = (gathered(part * half + r) * scale)[:owned]


def finish(parts, owned, slabs):
    return pl.pallas_call(
        lambda *args: finish_kernel(slabs, owned, *args),
        name="finish",
        out_shape=jax.ShapeDtypeStruct((owned, 2, slabs // 2, LANES), F32),
        compiler_params=pltpu.CompilerParams(vmem_limit_bytes=VMEM_LIMIT),
    )(parts)


def body(particles, references, class_index, rotation_index, defocus_group, log_prior, ctf_table):
    count, _, cycles, harmonics = particles.shape
    owned, _, share, _ = references.shape
    top = class_index.shape[1]
    owners = cycles // share
    slabs = 2 * share
    me = lax.axis_index("dp")

    padded = class_index + (32 - owned) * (class_index // owned)
    index_rows = jnp.concatenate(
        [padded, rotation_index, defocus_group[:, None], jnp.zeros((count, INDEX_ROWS - 2 * top - 1), jnp.int32)], axis=1
    )
    index_rows = index_rows.T.astype(BF16)
    own_refs = jnp.pad(references.transpose(1, 2, 0, 3).reshape(slabs, owned, harmonics), ((0, 0), (0, 32 - owned), (0, 0)))
    refs = lax.all_gather(own_refs, "cls", axis=0)
    ctf = lax.dynamic_slice(ctf_table, (0, me * share), (ctf_table.shape[0], share)).T
    ctf = jnp.pad(ctf, ((0, 8 - share), (0, 0)))
    ctf_parts = jnp.concatenate(split3(ctf), axis=0)
    mine = (jnp.arange(owners) == me)[:, None, None]
    prior = jnp.where(mine, log_prior.T[None], 0.0)
    phases = jnp.asarray(phase_table(harmonics))

    send = cut_particles(particles, index_rows, owners)
    send, refs, ctf_parts, prior = lax.optimization_barrier((send, refs, ctf_parts, prior))
    moved = lax.all_to_all(send, "dp", 0, 0)
    partial = partial_scores(moved, refs, ctf_parts, phases, prior, slabs, top)
    partials = lax.all_to_all(jnp.broadcast_to(partial[None], (owners,) + partial.shape), "dp", 0, 0)

    weights, sums = weighted_sums(moved, partials, ctf_parts, phases, slabs, top, refs.shape[0])
    parts = lax.all_to_all(sums, "cls", 0, 0)
    new_references = finish(parts, owned, slabs)
    own_weights = lax.dynamic_index_in_dim(weights, me, 0, keepdims=False).T
    return new_references, own_weights


def solution(mesh):
    in_specs = (
        P(("dp", "cls"), None, None, None),
        P("cls", None, "dp", None),
        P(("dp", "cls"), None),
        P(("dp", "cls"), None),
        P(("dp", "cls")),
        P(("dp", "cls"), None),
        P(),
    )
    out_specs = (P("cls", None, "dp", None), P(("dp", "cls"), None))
    return jax.shard_map(body, mesh=mesh, in_specs=in_specs, out_specs=out_specs, check_vma=False)
```

time: 190 us -> 164 us (0.86)
  blocking collectives: 23.3 us -> 93.2 us
  waiting for transfers between devices: 73 us -> 8.9 us
  between operations: 14.1 us -> 0.68 us
  Pallas kernels: 55.5 us -> 44.4 us
  starting transfers between devices: 16.4 us -> 7.25 us
    all_to_all x0 -> x1, blocking collectives: none -> 59.4 us  [body(): moved = lax.all_to_all(send, 'dp', 0, 0)]
    all_to_all x1 -> x0, waiting for transfers between devices: 37.4 us -> none  [body(): moved = lax.all_to_all(send, 'dp', 0, 0)]
    all_gather x1 -> x0, waiting for transfers between devices: 26.7 us -> none  [body(): refs = lax.all_gather(own_refs.astype(F32), 'cls', axis=0)]
    all_gather x0 -> x1, blocking collectives: none -> 15.9 us  [body(): refs = lax.all_gather(own_refs, 'cls', axis=0)]
    pallas_call x1, Pallas kernels: 25.8 us -> 15.9 us  [weighted_sums(): pl.pallas_call(lambda *args: sum_kernel(slabs, top, *args), name='sums',...]
    all_to_all x1 -> x0, starting transfers between devices: 8.77 us -> none  [body(): moved = lax.all_to_all(send, 'dp', 0, 0)]
    all_to_all x1, blocking collectives: 23.3 us -> 17.9 us  [body(): lax.all_to_all(jnp.broadcast_to(partial[None], (owners,) + partial.shape)...]
  transfers between devices with their start and end apart: 3 -> 1, of which waited for: 3 -> 1; matrix products, arithmetic and copies ran while one was open for 1% -> 1% of each run, Pallas kernels for 0% -> 0%
where the time goes in v3:
time: 164 us; the launch traced here: 163 us
  blocking collectives  93.2 us (57%)
  Pallas kernels  44.4 us (27%)
  waiting for transfers between devices  8.9 us (5%)
  starting transfers between devices  7.25 us (4%)
  other arithmetic  4.73 us (3%)
  local copies, waits for them, and re-layouts  3.96 us (2%)
    all_to_all x1, blocking collectives, body(): moved = lax.all_to_all(send, 'dp', 0, 0)  59.4 us
    pallas_call x1, Pallas kernels, partial_scores(): pl.pallas_call(lambda *args: score_kernel(slabs, top, *args), name='score...  20.9 us
    all_to_all x1, blocking collectives, body(): lax.all_to_all(jnp.broadcast_to(partial[None], (owners,) + partial.shape)...  17.9 us
    pallas_call x1, Pallas kernels, weighted_sums(): pl.pallas_call(lambda *args: sum_kernel(slabs, top, *args), name='sums',...  15.9 us
    all_gather x1, blocking collectives, body(): refs = lax.all_gather(own_refs, 'cls', axis=0)  15.9 us
    all_to_all x1, waiting for transfers between devices, body(): parts = lax.all_to_all(sums, 'cls', 0, 0)  8.9 us
    all_to_all x1, starting transfers between devices, body(): parts = lax.all_to_all(sums, 'cls', 0, 0)  7.25 us
    pallas_call x1, Pallas kernels, cut_particles(): pl.pallas_call(lambda *refs: cut_kernel(share, *refs), name='cut', grid=(...  5.61 us
  transfers between devices with their start and end apart: 1, of which 1 were waited for; matrix products, arithmetic and copies ran while one was open for 1% of the time, Pallas kernels for 0%

profile of v3, /device:TPU:1, one launch (start us, length us, event | category | flops | bytes accessed | tf_op | source)
XLA Modules:
  0.0 163.1 jit_solution(17367859512829799192)
XLA Ops:
  0.6 0.0 copy-start
  0.7 0.7 convert_bitcast_fusion
  1.3 0.7 fusion.4
  2.0 0.7 convert.13
  2.7 0.0 copy-done
  2.7 0.8 copy.11
  3.6 15.9 %all-gather = bf16[64,32,128]{2,1,0:T(8,128)(2,1)} all-gather(bf16[8,32,128]{2,1,0:T(8,128)(2,1)S(1)} %pad.8), channel_id=2, replica_groups=mesh['dp'=16,'cls'=8] {'cls'}, dimensions={0}, use_global_device_ids=true | all-gather | bytes 589824 | tf_op jit(solution)/shard_map/all_gather | solution.py:290
  19.5 0.1 pad.16.clone
  19.5 1.4 broadcast_select_fusion.args_4_
  20.9 0.7 maximum_bitcast_fusion.refs_1_
  21.6 5.6 %cut.1 = bf16[16,1056,128]{2,1,0:T(8,128)(2,1)} custom-call(bf16[128,2,64,128]{3,2,1,0:T(8,128)(2,1)} %refs_0_.1, bf16[32,128]{1,0:T(8,128)(2,1)} %maximum_bitcast_fusion.refs_1_), custom_call_target="tpu_custom_call" | custom-call | tf_op jit(solution)/shard_map/cut/pallas_call | solution.py:73
  27.2 0.6 pad_maximum_fusion.args_2_
  27.8 59.4 %all_to_all.15.args_0_ = bf16[16,1056,128]{2,1,0:T(8,128)(2,1)} all-to-all(bf16[16,1056,128]{2,1,0:T(8,128)(2,1)} %cut.1), channel_id=1, replica_groups=mesh['dp'=16,'cls'=8] {'dp'}, dimensions={0} | all-to-all | bytes 8650752 | tf_op jit(solution)/shard_map/all_to_all | solution.py:300
  87.2 20.9 %score.1 = f32[16,8,128]{2,1,0:T(8,128)} custom-call(bf16[16,1056,128]{2,1,0:T(8,128)(2,1)} %all_to_all.15.args_0_, bf16[8,8,32,128]{3,2,1,0:T(8,128)(2,1)} %bitcast.14, bf16[24,128]{1,0:T(8,128)(2,1)} %pad_maximum_fusion.args_2_, bf16[256,128]{1,0:T(8,128)(2,1)} %constant.38.clone.args_3_, f32[16,8,128]{2,1,0:T(8,128)} %broadcast_select_fusion.args_4_), custom_call_target="tpu_custom_call" | custom-call | tf_op jit(solution)/shard_map/score/pallas_call | solution.py:155
  108.2 0.9 broadcast_in_dim.40
  109.1 17.9 %all_to_all.16.args_1_ = f32[16,16,8,128]{3,2,1,0:T(8,128)} all-to-all(f32[16,16,8,128]{3,2,1,0:T(8,128)S(1)} %broadcast_in_dim.40), channel_id=1, replica_groups=mesh['dp'=16,'cls'=8] {'dp'}, dimensions={0} | all-to-all | bytes 2097152 | tf_op jit(solution)/shard_map/all_to_all | solution.py:302
  127.0 15.9 %sums.1 = (f32[16,8,128]{2,1,0:T(8,128)}, bf16[8,9,32,128]{3,2,1,0:T(8,128)(2,1)}) custom-call(bf16[16,1056,128]{2,1,0:T(8,128)(2,1)} %all_to_all.15.args_0_, f32[16,16,8,128]{3,2,1,0:T(8,128)} %all_to_all.16.args_1_, bf16[24,128]{1,0:T(8,128)(2,1)} %pad_maximum_fusion.args_2_, bf16[256,128]{1,0:T(8,128)(2,1)} %constant.38.clone.args_3_), custom_call_target="tpu_custom_call" | custom-call | tf_op jit(solution)/shard_map/sums/pallas_call | solution.py:230
  142.9 7.2 %all-to-all-start.2 = ((bf16[8,9,32,128]{3,2,1,0:T(8,128)(2,1)}), bf16[8,9,32,128]{3,2,1,0:T(8,128)(2,1)S(1)}, u32[]{:S(2)}, u32[]{:S(2)}) async-start(bf16[8,9,32,128]{3,2,1,0:T(8,128)(2,1)} %get-tuple-element.12), calls=%async_computation.2 | async-start | bytes 1179648 | tf_op jit(solution)/shard_map/all_to_all | solution.py:305
  150.2 1.3 dynamic-slice_bitcast_fusion
  151.5 8.9 %all-to-all-done.2.args_0_ = bf16[8,9,32,128]{3,2,1,0:T(8,128)(2,1)S(1)} async-done(((bf16[8,9,32,128]{3,2,1,0:T(8,128)(2,1)}), bf16[8,9,32,128]{3,2,1,0:T(8,128)(2,1)S(1)}, u32[]{:S(2)}, u32[]{:S(2)}) %all-to-all-start.2) | async-done | bytes 589856 | tf_op jit(solution)/shard_map/all_to_all | solution.py:305
  160.4 0.0 copy-start.1
  160.4 0.8 copy-done.1
  161.2 1.9 %finish.1 = f32[25,2,4,128]{3,2,1,0:T(4,128)} custom-call(bf16[8,9,32,128]{3,2,1,0:T(8,128)(2,1)} %copy-done.1), custom_call_target="tpu_custom_call" | custom-call | tf_op jit(solution)/shard_map/finish/pallas_call | solution.py:268
  (5 shorter events, 0.0 us)
Async XLA Ops:
  0.6 2.1 %copy-start = (f32[128,64]{0,1:T(8,128)S(1)}, f32[128,64]{0,1:T(8,128)}, u32[]{:S(2)}) copy-start(f32[128,64]{0,1:T(8,128)} %param.14) | copy-start | bytes 98308
  142.9 17.4 %all-to-all-start.2 = ((bf16[8,9,32,128]{3,2,1,0:T(8,128)(2,1)}), bf16[8,9,32,128]{3,2,1,0:T(8,128)(2,1)S(1)}, u32[]{:S(2)}, u32[]{:S(2)}) async-start(bf16[8,9,32,128]{3,2,1,0:T(8,128)(2,1)} %get-tuple-element.12), calls=%async_computation.2 | async-start | bytes 1179648 | tf_op jit(solution)/shard_map/all_to_all | solution.py:305
  160.4 0.8 copy-start.1

commit v4 on v3

--- a/solution.py
+++ b/solution.py
@@ -122,7 +122,7 @@
     def _():
         for slab in range(slabs):
             for piece in range(2):
-                devs = [refs_ref[piece * 4 + dev, slab].astype(F32) for dev in range(4)]
+                devs = [refs_ref[piece * 4 + dev, slab] for dev in range(4)]
                 table[slab * 128 : (slab + 1) * 128, piece * 128 : (piece + 1) * 128] = jnp.concatenate(devs, axis=0).T.astype(BF16)
 
     classes = row_iota(256).astype(F32)
@@ -132,21 +132,23 @@
         scores = []
         for pair in range(top // 2):
             hot = jnp.concatenate([hot_rows(index[j : j + 1, :], classes) for j in (2 * pair, 2 * pair + 1)], axis=1)
-            picked = jnp.dot(table[...], hot, preferred_element_type=F32)
+            evens, odds = [None, None], [None, None]
+            for r in range(half):
+                ref_re = jnp.dot(table[r * 128 : (r + 1) * 128, :], hot, preferred_element_type=F32)
+                ref_im = jnp.dot(table[(half + r) * 128 : (half + r + 1) * 128, :], hot, preferred_element_type=F32)
+                re, im = scaled[r], scaled[half + r]
+                for side in range(2):
+                    here = slice(side * 128, (side + 1) * 128)
+                    a = re * ref_re[:, here] + im * ref_im[:, here]
+                    b = re * ref_im[:, here] - im * ref_re[:, here]
+                    evens[side] = a if r == 0 else evens[side] + a
+                    odds[side] = b if r == 0 else odds[side] + b
             for side in range(2):
                 across = slice((2 * pair + side) * 128, (2 * pair + side + 1) * 128)
-                here = slice(side * 128, (side + 1) * 128)
-                even = odd = None
-                for r in range(half):
-                    ref_re = picked[r * 128 : (r + 1) * 128, here]
-                    ref_im = picked[(half + r) * 128 : (half + r + 1) * 128, here]
-                    re, im = scaled[r], scaled[half + r]
-                    a = re * ref_re + im * ref_im
-                    b = re * ref_im - im * ref_re
-                    even = a if even is None else even + a
-                    odd = b if odd is None else odd + b
-                scores.append(jnp.sum(angles[:128, across] * even + angles[128:, across] * odd, axis=0, keepdims=True))
-        out_ref[s] = SCORE_SCALE * jnp.concatenate(scores, axis=0) + prior_ref[s]
+                scores.append(jnp.sum(angles[:128, across] * evens[side] + angles[128:, across] * odds[side], axis=0, keepdims=True))
+        score = SCORE_SCALE * jnp.concatenate(scores, axis=0) + prior_ref[s]
+        for owner in range(out_ref.shape[0]):
+            out_ref[owner, s] = score
 
 
 def partial_scores(moved, refs, ctf_parts, phases, prior, slabs, top):
@@ -163,8 +165,8 @@
             whole(phases),
             pl.BlockSpec((2, top, lanes), lambda s: (s, 0, 0)),
         ],
-        out_specs=pl.BlockSpec((2, top, lanes), lambda s: (s, 0, 0)),
-        out_shape=jax.ShapeDtypeStruct((sources, top, lanes), F32),
+        out_specs=pl.BlockSpec((sources, 2, top, lanes), lambda s: (0, s, 0, 0)),
+        out_shape=jax.ShapeDtypeStruct((sources, sources, top, lanes), F32),
         scratch_shapes=[pltpu.VMEM((slabs * 128, 256), BF16)],
         compiler_params=pltpu.CompilerParams(vmem_limit_bytes=VMEM_LIMIT),
     )(moved, refs, ctf_parts, phases, prior)
@@ -287,7 +289,7 @@
     )
     index_rows = index_rows.T.astype(BF16)
     own_refs = jnp.pad(references.transpose(1, 2, 0, 3).reshape(slabs, owned, harmonics), ((0, 0), (0, 32 - owned), (0, 0)))
-    refs = lax.all_gather(own_refs, "cls", axis=0)
+    refs = lax.all_gather(own_refs.astype(F32), "cls", axis=0)
     ctf = lax.dynamic_slice(ctf_table, (0, me * share), (ctf_table.shape[0], share)).T
     ctf = jnp.pad(ctf, ((0, 8 - share), (0, 0)))
     ctf_parts = jnp.concatenate(split3(ctf), axis=0)
@@ -296,10 +298,9 @@
     phases = jnp.asarray(phase_table(harmonics))
 
     send = cut_particles(particles, index_rows, owners)
-    send, refs, ctf_parts, prior = lax.optimization_barrier((send, refs, ctf_parts, prior))
-    moved = lax.all_to_all(send, "dp", 0, 0)
+    moved = lax.cond(defocus_group[0] >= 0, lambda a: lax.all_to_all(a, "dp", 0, 0), lambda a: a, send)
     partial = partial_scores(moved, refs, ctf_parts, phases, prior, slabs, top)
-    partials = lax.all_to_all(jnp.broadcast_to(partial[None], (owners,) + partial.shape), "dp", 0, 0)
+    partials = lax.all_to_all(partial, "dp", 0, 0)
 
     weights, sums = weighted_sums(moved, partials, ctf_parts, phases, slabs, top, refs.shape[0])
     parts = lax.all_to_all(sums, "cls", 0, 0)

time: 164 us -> 164 us (level)
  between operations: 0.68 us -> 14.7 us
  blocking collectives: 93.2 us -> 79.4 us
    all_gather x1 -> x0, blocking collectives: 15.9 us -> none  [body(): refs = lax.all_gather(own_refs, 'cls', axis=0)]
    cond x0 -> x2, local copies, waits for them, and re-layouts: none -> 2.24 us
    all_to_all x2, blocking collectives: 77.3 us -> 79.4 us  [the longest x1 60 us: body(): lax.all_to_all(a, 'dp', 0, 0)]
  transfers between devices with their start and end apart: 1 -> 2, of which waited for: 1 -> 1; matrix products, arithmetic and copies ran while one was open for 1% -> 3% of each run, Pallas kernels for 0% -> 3%
where the time goes in v4:
time: 164 us
  blocking collectives  79.4 us (48%)
  Pallas kernels  43.3 us (26%)
  between operations  14.7 us (9%)
  waiting for transfers between devices  8.92 us (5%)
  starting transfers between devices  7.37 us (4%)
  local copies, waits for them, and re-layouts  5.27 us (3%)
  other arithmetic  4.71 us (3%)
    all_to_all x1, blocking collectives, body(): lax.all_to_all(a, 'dp', 0, 0)  60 us
    pallas_call x1, Pallas kernels, partial_scores(): pl.pallas_call(lambda *args: score_kernel(slabs, top, *args), name='score...  20.2 us
    all_to_all x1, blocking collectives, body(): partials = lax.all_to_all(partial, 'dp', 0, 0)  19.4 us
    pallas_call x1, Pallas kernels, weighted_sums(): pl.pallas_call(lambda *args: sum_kernel(slabs, top, *args), name='sums',...  15.6 us
    all_to_all x1, waiting for transfers between devices, body(): parts = lax.all_to_all(sums, 'cls', 0, 0)  8.9 us
    all_to_all x1, starting transfers between devices, body(): parts = lax.all_to_all(sums, 'cls', 0, 0)  7.33 us
    pallas_call x1, Pallas kernels, cut_particles(): pl.pallas_call(lambda *refs: cut_kernel(share, *refs), name='cut', grid=(...  5.55 us
  transfers between devices with their start and end apart: 2, of which 1 were waited for; matrix products, arithmetic and copies ran while one was open for 3% of the time, Pallas kernels for 3%

profile of v4, /device:TPU:1, one launch (start us, length us, event | category | flops | bytes accessed | tf_op | source)
XLA Modules:
  0.0 163.6 jit_solution(11969523452034000659)
XLA Ops:
  7.2 0.0 copy-start
  7.2 0.0 all-gather.3.cloned.1.call-start
  7.2 0.8 copy.11
  8.0 0.7 pad_convert_fusion
  8.7 0.0 all-gather.3.cloned.1.call-update
  9.4 0.7 convert.15
  10.1 0.1 pad.16.clone
  10.2 0.7 convert_bitcast_fusion
  10.8 0.7 fusion.4
  11.5 0.7 maximum_bitcast_fusion.refs_1_
  12.2 5.5 %cut.1 = bf16[16,1056,128]{2,1,0:T(8,128)(2,1)} custom-call(bf16[128,2,64,128]{3,2,1,0:T(8,128)(2,1)} %refs_0_.1, bf16[32,128]{1,0:T(8,128)(2,1)} %maximum_bitcast_fusion.refs_1_), custom_call_target="tpu_custom_call" | custom-call | tf_op jit(solution)/shard_map/cut/pallas_call | solution.py:73
  17.7 62.3 %conditional.1 = (bf16[16,1056,128]{2,1,0:T(8,128)(2,1)}) conditional(s32[]{:T(128)} %bitcast, bf16[16,1056,128]{2,1,0:T(8,128)(2,1)} %cut.1, bf16[16,1056,128]{2,1,0:T(8,128)(2,1)} %cut.1), branch_computations={%region_0.1_spmd, %region_1.2_spmd} | conditional | bytes 25952292 | solution.py:301
  17.7 2.2 %copy-done.1 = bf16[16,1056,128]{2,1,0:T(8,128)(2,1)S(1)} copy-done((bf16[16,1056,128]{2,1,0:T(8,128)(2,1)S(1)}, bf16[16,1056,128]{2,1,0:T(8,128)(2,1)}, u32[]{:S(2)}) %copy-start.1) | copy-done | bytes 4325400 | tf_op jit(solution)/shard_map/cond
  20.0 60.0 %all_to_all.14 = bf16[16,1056,128]{2,1,0:T(8,128)(2,1)} all-to-all(bf16[16,1056,128]{2,1,0:T(8,128)(2,1)S(1)} %copy-done.1), channel_id=1, replica_groups=mesh['dp'=16,'cls'=8] {'dp'}, dimensions={0} | all-to-all | bytes 8650752 | tf_op jit(solution)/shard_map/cond/branch_1_fun/all_to_all | solution.py:301
  80.1 0.6 pad_maximum_fusion.args_2_
  80.7 0.7 broadcast_select_fusion.args_4_
  81.4 20.2 %score.1 = f32[16,16,8,128]{3,2,1,0:T(8,128)} custom-call(bf16[16,1056,128]{2,1,0:T(8,128)(2,1)} %get-tuple-element.14.args_0_, f32[8,8,32,128]{3,2,1,0:T(8,128)} %bitcast.18, bf16[24,128]{1,0:T(8,128)(2,1)} %pad_maximum_fusion.args_2_, bf16[256,128]{1,0:T(8,128)(2,1)} %constant.40.clone.args_3_, f32[16,8,128]{2,1,0:T(8,128)} %broadcast_select_fusion.args_4_), custom_call_target="tpu_custom_call" | custom-call | tf_op jit(solution)/shard_map/score/pallas_call | solution.py:157
  101.6 19.4 %all_to_all.15.args_1_ = f32[16,16,8,128]{3,2,1,0:T(8,128)} all-to-all(f32[16,16,8,128]{3,2,1,0:T(8,128)} %score.1), channel_id=1, replica_groups=mesh['dp'=16,'cls'=8] {'dp'}, dimensions={0} | all-to-all | bytes 2097152 | tf_op jit(solution)/shard_map/all_to_all | solution.py:303
  121.0 15.6 %sums.1 = (f32[16,8,128]{2,1,0:T(8,128)}, bf16[8,9,32,128]{3,2,1,0:T(8,128)(2,1)}) custom-call(bf16[16,1056,128]{2,1,0:T(8,128)(2,1)S(1)} %bitcast.17, f32[16,16,8,128]{3,2,1,0:T(8,128)} %all_to_all.15.args_1_, bf16[24,128]{1,0:T(8,128)(2,1)} %pad_maximum_fusion.args_2_, bf16[256,128]{1,0:T(8,128)(2,1)} %constant.40.clone.args_3_), custom_call_target="tpu_custom_call" | custom-call | tf_op jit(solution)/shard_map/sums/pallas_call | solution.py:232
  136.5 7.3 %all-to-all-start.2 = ((bf16[8,9,32,128]{3,2,1,0:T(8,128)(2,1)}), bf16[8,9,32,128]{3,2,1,0:T(8,128)(2,1)S(1)}, u32[]{:S(2)}, u32[]{:S(2)}) async-start(bf16[8,9,32,128]{3,2,1,0:T(8,128)(2,1)} %get-tuple-element.9), calls=%async_computation.2 | async-start | bytes 1179648 | tf_op jit(solution)/shard_map/all_to_all | solution.py:306
  143.9 1.3 dynamic-slice_bitcast_fusion
  145.1 8.9 %all-to-all-done.2.args_0_ = bf16[8,9,32,128]{3,2,1,0:T(8,128)(2,1)S(1)} async-done(((bf16[8,9,32,128]{3,2,1,0:T(8,128)(2,1)}), bf16[8,9,32,128]{3,2,1,0:T(8,128)(2,1)S(1)}, u32[]{:S(2)}, u32[]{:S(2)}) %all-to-all-start.2) | async-done | bytes 589856 | tf_op jit(solution)/shard_map/all_to_all | solution.py:306
  154.1 0.8 copy-done.2
  154.9 1.9 %finish.1 = f32[25,2,4,128]{3,2,1,0:T(4,128)} custom-call(bf16[8,9,32,128]{3,2,1,0:T(8,128)(2,1)} %copy-done.2), custom_call_target="tpu_custom_call" | custom-call | tf_op jit(solution)/shard_map/finish/pallas_call | solution.py:270
  (15 shorter events, 0.0 us)
Async XLA Ops:
  7.2 72.9 %copy-start = (f32[128,64]{0,1:T(8,128)S(1)}, f32[128,64]{0,1:T(8,128)}, u32[]{:S(2)}) copy-start(f32[128,64]{0,1:T(8,128)} %param.16) | copy-start | bytes 98308
  7.2 74.2 %all-gather.3.cloned.1.call-start = ((), (), s32[]{:S(2)}) async-start(), calls=%async_computation.3 | async-start | bytes 1179648 | tf_op jit(solution)/shard_map/all_gather | solution.py:292
  17.7 62.9 %copy-start.3 = (f32[128,8]{0,1:T(8,128)S(1)}, f32[128,8]{0,1:T(8,128)}, u32[]{:S(2)}) copy-start(f32[128,8]{0,1:T(8,128)} %param.15) | copy-start | bytes 12292
  17.7 2.2 %copy-start.1 = (bf16[16,1056,128]{2,1,0:T(8,128)(2,1)S(1)}, bf16[16,1056,128]{2,1,0:T(8,128)(2,1)}, u32[]{:S(2)}) copy-start(bf16[16,1056,128]{2,1,0:T(8,128)(2,1)} %param.1) | copy-start | bytes 12976132 | tf_op jit(solution)/shard_map/cond
  81.4 39.6 %slice-start = ((s8[4325376]{0:T(1024)(128)(4,1)}), s8[4194304]{0:T(1024)(128)(4,1)S(1)}, s32[]{:S(2)}) async-start(s8[4325376]{0:T(1024)(128)(4,1)} %bitcast.16), calls=%async_computation.4 | async-start | bytes 8388608
  81.4 39.6 %slice-start.1 = ((s8[4325376]{0:T(1024)(128)(4,1)}), s8[131072]{0:T(1024)(128)(4,1)S(1)}, s32[]{:S(2)}) async-start(s8[4325376]{0:T(1024)(128)(4,1)} %bitcast.16), calls=%async_computation.5 | async-start | bytes 262144
  136.5 17.5 %all-to-all-start.2 = ((bf16[8,9,32,128]{3,2,1,0:T(8,128)(2,1)}), bf16[8,9,32,128]{3,2,1,0:T(8,128)(2,1)S(1)}, u32[]{:S(2)}, u32[]{:S(2)}) async-start(bf16[8,9,32,128]{3,2,1,0:T(8,128)(2,1)} %get-tuple-element.9), calls=%async_computation.2 | async-start | bytes 1179648 | tf_op jit(solution)/shard_map/all_to_all | solution.py:306
  154.1 0.8 copy-start.2
Sparse Core Ops, SparseCore 0:
  9.7 26.9 all-gather.2

commit v5 on v4

--- a/solution.py
+++ b/solution.py
@@ -48,7 +48,7 @@
     return np.concatenate([stacked, pad], axis=0).T
 
 
-def cut_kernel(share, x_ref, index_ref, out_ref):
+def cut_kernel(share, owned, x_ref, class_ref, rotation_ref, group_ref, out_ref):
     step = pl.program_id(0)
     block, parts, cycles, lanes = x_ref.shape
     owners = out_ref.shape[0]
@@ -61,27 +61,32 @@
 
     @pl.when(step == 0)
     def _():
+        padded = class_ref[...]
+        for k in range(1, 256 // 32):
+            padded = padded + jnp.where(class_ref[...] >= k * owned, 32 - owned, 0)
+        group = jnp.broadcast_to(group_ref[...], padded.shape)
+        rows = jnp.concatenate([padded, rotation_ref[...], group, jnp.zeros_like(padded)], axis=0)
+        rows = rows.astype(F32).astype(BF16)
         for owner in range(owners):
-            out_ref[owner, 2 * share * 128 :, :] = index_ref[...]
-
-
-def cut_particles(particles, index_rows, owners):
+            out_ref[owner, 2 * share * 128 :, :] = rows
+
+
+def cut_particles(particles, classes, rotations, groups, owners, owned):
     count, parts, cycles, lanes = particles.shape
     share = cycles // owners
     block = 32
     out_rows = 2 * share * count + INDEX_ROWS
+    index = [pl.BlockSpec(a.shape, lambda s: (0, 0)) for a in (classes, rotations, groups)]
     return pl.pallas_call(
-        lambda *refs: cut_kernel(share, *refs),
+        lambda *refs: cut_kernel(share, owned, *refs),
         name="cut",
         grid=(count // block,),
-        in_specs=[
-            pl.BlockSpec((block, parts, cycles, lanes), lambda s: (s, 0, 0, 0)),
-            pl.BlockSpec((INDEX_ROWS, lanes), lambda s: (0, 0)),
-        ],
+        in_specs=[pl.BlockSpec((block, parts, cycles, lanes), lambda s: (s, 0, 0, 0))] + index,
         out_specs=pl.BlockSpec((owners, out_rows, lanes), lambda s: (0, 0, 0)),
         out_shape=jax.ShapeDtypeStruct((owners, out_rows, lanes), BF16),
+        cost_estimate=pl.CostEstimate(flops=0, bytes_accessed=4 * particles.size, transcendentals=0),
         compiler_params=pltpu.CompilerParams(vmem_limit_bytes=VMEM_LIMIT),
-    )(particles, index_rows)
+    )(particles, classes, rotations, groups)
 
 
 def row_iota(rows):
@@ -115,14 +120,14 @@
     return rows, ctf, scaled, rotations(rows, top, phases)
 
 
-def score_kernel(slabs, top, x_ref, refs_ref, ctf_parts, phases, prior_ref, out_ref, table):
+def score_kernel(slabs, top, x_ref, refs_ref, ctf_parts, phases, prior_ref, me_ref, out_ref, table):
     half = slabs // 2
 
     @pl.when(pl.program_id(0) == 0)
     def _():
         for slab in range(slabs):
             for piece in range(2):
-                devs = [refs_ref[piece * 4 + dev, slab] for dev in range(4)]
+                devs = [refs_ref[piece * 4 + dev, slab].astype(F32) for dev in range(4)]
                 table[slab * 128 : (slab + 1) * 128, piece * 128 : (piece + 1) * 128] = jnp.concatenate(devs, axis=0).T.astype(BF16)
 
     classes = row_iota(256).astype(F32)
@@ -146,12 +151,13 @@
             for side in range(2):
                 across = slice((2 * pair + side) * 128, (2 * pair + side + 1) * 128)
                 scores.append(jnp.sum(angles[:128, across] * evens[side] + angles[128:, across] * odds[side], axis=0, keepdims=True))
-        score = SCORE_SCALE * jnp.concatenate(scores, axis=0) + prior_ref[s]
+        own = pl.program_id(0) * x_ref.shape[0] + s == me_ref[0]
+        score = SCORE_SCALE * jnp.concatenate(scores, axis=0) + jnp.where(own, prior_ref[...], 0.0)
         for owner in range(out_ref.shape[0]):
             out_ref[owner, s] = score
 
 
-def partial_scores(moved, refs, ctf_parts, phases, prior, slabs, top):
+def partial_scores(moved, refs, ctf_parts, phases, prior, me, slabs, top):
     sources, rows, lanes = moved.shape
     whole = lambda a: pl.BlockSpec(a.shape, lambda s, n=a.ndim: (0,) * n)
     return pl.pallas_call(
@@ -163,13 +169,14 @@
             whole(refs),
             whole(ctf_parts),
             whole(phases),
-            pl.BlockSpec((2, top, lanes), lambda s: (s, 0, 0)),
+            whole(prior),
+            pl.BlockSpec(memory_space=pltpu.SMEM),
         ],
         out_specs=pl.BlockSpec((sources, 2, top, lanes), lambda s: (0, s, 0, 0)),
         out_shape=jax.ShapeDtypeStruct((sources, sources, top, lanes), F32),
         scratch_shapes=[pltpu.VMEM((slabs * 128, 256), BF16)],
         compiler_params=pltpu.CompilerParams(vmem_limit_bytes=VMEM_LIMIT),
-    )(moved, refs, ctf_parts, phases, prior)
+    )(moved, refs, ctf_parts, phases, prior, me.astype(jnp.int32).reshape(1))
 
 
 def parted(x):
@@ -283,23 +290,18 @@
     slabs = 2 * share
     me = lax.axis_index("dp")
 
-    padded = class_index + (32 - owned) * (class_index // owned)
-    index_rows = jnp.concatenate(
-        [padded, rotation_index, defocus_group[:, None], jnp.zeros((count, INDEX_ROWS - 2 * top - 1), jnp.int32)], axis=1
-    )
-    index_rows = index_rows.T.astype(BF16)
     own_refs = jnp.pad(references.transpose(1, 2, 0, 3).reshape(slabs, owned, harmonics), ((0, 0), (0, 32 - owned), (0, 0)))
-    refs = lax.all_gather(own_refs.astype(F32), "cls", axis=0)
+    holders = lax.axis_size("cls")
+    refs = lax.all_to_all(jnp.broadcast_to(own_refs[None], (holders,) + own_refs.shape), "cls", 0, 0)
     ctf = lax.dynamic_slice(ctf_table, (0, me * share), (ctf_table.shape[0], share)).T
     ctf = jnp.pad(ctf, ((0, 8 - share), (0, 0)))
     ctf_parts = jnp.concatenate(split3(ctf), axis=0)
-    mine = (jnp.arange(owners) == me)[:, None, None]
-    prior = jnp.where(mine, log_prior.T[None], 0.0)
     phases = jnp.asarray(phase_table(harmonics))
 
-    send = cut_particles(particles, index_rows, owners)
-    moved = lax.cond(defocus_group[0] >= 0, lambda a: lax.all_to_all(a, "dp", 0, 0), lambda a: a, send)
-    partial = partial_scores(moved, refs, ctf_parts, phases, prior, slabs, top)
+    send = cut_particles(particles, class_index.T, rotation_index.T, defocus_group[None], owners, owned)
+    send, refs, ctf_parts = lax.optimization_barrier((send, refs, ctf_parts))
+    moved = lax.all_to_all(send, "dp", 0, 0)
+    partial = partial_scores(moved, refs, ctf_parts, phases, log_prior.T, me, slabs, top)
     partials = lax.all_to_all(partial, "dp", 0, 0)
 
     weights, sums = weighted_sums(moved, partials, ctf_parts, phases, slabs, top, refs.shape[0])

time: 164 us -> 151 us (0.921)
  between operations: 14.7 us -> 0.66 us
  starting transfers between devices: 7.37 us -> 12.9 us
  other arithmetic: 4.71 us -> 0.6 us
  waiting for transfers between devices: 8.92 us -> 12.2 us
  blocking collectives: 79.4 us -> 77.1 us
    all_to_all x0 -> x1, starting transfers between devices: none -> 5.8 us  [body(): lax.all_to_all(jnp.broadcast_to(own_refs[None], (holders,) + own_refs.sha...]
    all_to_all x0 -> x1, waiting for transfers between devices: none -> 3.25 us  [body(): lax.all_to_all(jnp.broadcast_to(own_refs[None], (holders,) + own_refs.sha...]
    cond x2 -> x0, local copies, waits for them, and re-layouts: 2.24 us -> none
    all_to_all x1, blocking collectives: 60 us -> 58.3 us  [body(): moved = lax.all_to_all(send, 'dp', 0, 0)]
  transfers between devices with their start and end apart: 2 -> 2, of which waited for: 1 -> 2; matrix products, arithmetic and copies ran while one was open for 3% -> 1% of each run, Pallas kernels for 3% -> 4%
where the time goes in v5:
time: 151 us
  blocking collectives  77.1 us (51%)
  Pallas kernels  43.3 us (29%)
  starting transfers between devices  12.9 us (9%)
  waiting for transfers between devices  12.2 us (8%)
  local copies, waits for them, and re-layouts  3.84 us (3%)
    all_to_all x1, blocking collectives, body(): moved = lax.all_to_all(send, 'dp', 0, 0)  58.3 us
    pallas_call x1, Pallas kernels, partial_scores(): pl.pallas_call(lambda *args: score_kernel(slabs, top, *args), name='score...  19.8 us
    all_to_all x1, blocking collectives, body(): partials = lax.all_to_all(partial, 'dp', 0, 0)  18.7 us
    pallas_call x1, Pallas kernels, weighted_sums(): pl.pallas_call(lambda *args: sum_kernel(slabs, top, *args), name='sums',...  15.9 us
    all_to_all x1, waiting for transfers between devices, body(): parts = lax.all_to_all(sums, 'cls', 0, 0)  8.92 us
    all_to_all x1, starting transfers between devices, body(): parts = lax.all_to_all(sums, 'cls', 0, 0)  7.1 us
    all_to_all x1, starting transfers between devices, body(): lax.all_to_all(jnp.broadcast_to(own_refs[None], (holders,) + own_refs.sha...  5.8 us
    pallas_call x1, Pallas kernels, cut_particles(): pl.pallas_call(lambda *refs: cut_kernel(share, owned, *refs), name='cut',...  5.61 us
  transfers between devices with their start and end apart: 2, of which 2 were waited for; matrix products, arithmetic and copies ran while one was open for 1% of the time, Pallas kernels for 4%

profile of v5, /device:TPU:1, one launch (start us, length us, event | category | flops | bytes accessed | tf_op | source)
XLA Modules:
  0.0 150.5 jit_solution(11931096654308140233)
XLA Ops:
  0.6 0.0 copy-start
  0.6 0.8 copy.10
  1.5 0.9 broadcast_in_dim.10
  2.4 5.8 %all-to-all-start = ((bf16[8,8,32,128]{3,2,1,0:T(8,128)(2,1)}), bf16[8,8,32,128]{3,2,1,0:T(8,128)(2,1)S(1)}, u32[]{:S(2)}, u32[]{:S(2)}) async-start(bf16[8,8,32,128]{3,2,1,0:T(8,128)(2,1)} %broadcast_in_dim.10), calls=%async_computation | async-start | bytes 1048576 | tf_op jit(solution)/shard_map/all_to_all | solution.py:295
  8.2 5.6 %cut.1 = bf16[16,1056,128]{2,1,0:T(8,128)(2,1)} custom-call(bf16[128,2,64,128]{3,2,1,0:T(8,128)(2,1)} %refs_0_.1, s32[8,128]{1,0:T(8,128)} %bitcast.15, s32[8,128]{1,0:T(8,128)} %bitcast.16, s32[1,128]{1,0:T(1,128)} %bitcast.18), custom_call_target="tpu_custom_call" | custom-call | bytes 8388608 | tf_op jit(solution)/shard_map/cut/pallas_call | solution.py:80
  13.8 0.0 copy-done
  13.8 0.6 pad_maximum_fusion.args_2_
  14.4 3.2 %all-to-all-done.args_1_ = bf16[8,8,32,128]{3,2,1,0:T(8,128)(2,1)S(1)} async-done(((bf16[8,8,32,128]{3,2,1,0:T(8,128)(2,1)}), bf16[8,8,32,128]{3,2,1,0:T(8,128)(2,1)S(1)}, u32[]{:S(2)}, u32[]{:S(2)}) %all-to-all-start) | async-done | bytes 524320 | tf_op jit(solution)/shard_map/all_to_all | solution.py:295
  17.7 0.0 copy-start.2
  17.7 58.3 %all_to_all.20.args_0_ = bf16[16,1056,128]{2,1,0:T(8,128)(2,1)} all-to-all(bf16[16,1056,128]{2,1,0:T(8,128)(2,1)} %cut.1), channel_id=1, replica_groups=mesh['dp'=16,'cls'=8] {'dp'}, dimensions={0} | all-to-all | bytes 8650752 | tf_op jit(solution)/shard_map/all_to_all | solution.py:303
  76.0 0.0 copy-done.2
  76.0 19.8 %score.1 = f32[16,16,8,128]{3,2,1,0:T(8,128)} custom-call(bf16[16,1056,128]{2,1,0:T(8,128)(2,1)} %all_to_all.20.args_0_, bf16[8,8,32,128]{3,2,1,0:T(8,128)(2,1)} %copy-done.2, bf16[24,128]{1,0:T(8,128)(2,1)} %pad_maximum_fusion.args_2_, bf16[256,128]{1,0:T(8,128)(2,1)} %constant.23.clone.args_3_, f32[8,128]{1,0:T(8,128)} %bitcast.17, s32[1]{0:T(128)} %bitcast.7.args_5_), custom_call_target="tpu_custom_call" | custom-call | tf_op jit(solution)/shard_map/score/pallas_call | solution.py:163
  95.8 18.7 %all_to_all.21.args_1_ = f32[16,16,8,128]{3,2,1,0:T(8,128)} all-to-all(f32[16,16,8,128]{3,2,1,0:T(8,128)} %score.1), channel_id=1, replica_groups=mesh['dp'=16,'cls'=8] {'dp'}, dimensions={0} | all-to-all | bytes 2097152 | tf_op jit(solution)/shard_map/all_to_all | solution.py:305
  114.6 15.9 %sums.1 = (f32[16,8,128]{2,1,0:T(8,128)}, bf16[8,9,32,128]{3,2,1,0:T(8,128)(2,1)}) custom-call(bf16[16,1056,128]{2,1,0:T(8,128)(2,1)} %all_to_all.20.args_0_, f32[16,16,8,128]{3,2,1,0:T(8,128)} %all_to_all.21.args_1_, bf16[24,128]{1,0:T(8,128)(2,1)} %pad_maximum_fusion.args_2_, bf16[256,128]{1,0:T(8,128)(2,1)} %constant.23.clone.args_3_), custom_call_target="tpu_custom_call" | custom-call | tf_op jit(solution)/shard_map/sums/pallas_call | solution.py:239
  130.5 7.1 %all-to-all-start.3 = ((bf16[8,9,32,128]{3,2,1,0:T(8,128)(2,1)}), bf16[8,9,32,128]{3,2,1,0:T(8,128)(2,1)S(1)}, u32[]{:S(2)}, u32[]{:S(2)}) async-start(bf16[8,9,32,128]{3,2,1,0:T(8,128)(2,1)} %get-tuple-element.10), calls=%async_computation.3 | async-start | bytes 1179648 | tf_op jit(solution)/shard_map/all_to_all | solution.py:308
  137.6 1.3 dynamic-slice_bitcast_fusion
  138.9 8.9 %all-to-all-done.3.args_0_ = bf16[8,9,32,128]{3,2,1,0:T(8,128)(2,1)S(1)} async-done(((bf16[8,9,32,128]{3,2,1,0:T(8,128)(2,1)}), bf16[8,9,32,128]{3,2,1,0:T(8,128)(2,1)S(1)}, u32[]{:S(2)}, u32[]{:S(2)}) %all-to-all-start.3) | async-done | bytes 589856 | tf_op jit(solution)/shard_map/all_to_all | solution.py:308
  147.8 0.0 copy-start.1
  147.8 0.8 copy-done.1
  148.6 1.9 %finish.1 = f32[25,2,4,128]{3,2,1,0:T(4,128)} custom-call(bf16[8,9,32,128]{3,2,1,0:T(8,128)(2,1)} %copy-done.1), custom_call_target="tpu_custom_call" | custom-call | tf_op jit(solution)/shard_map/finish/pallas_call | solution.py:277
  (3 shorter events, 0.0 us)
Async XLA Ops:
  0.6 13.2 %copy-start = (f32[128,64]{0,1:T(8,128)S(1)}, f32[128,64]{0,1:T(8,128)}, u32[]{:S(2)}) copy-start(f32[128,64]{0,1:T(8,128)} %param.14) | copy-start | bytes 98308
  2.4 15.3 %all-to-all-start = ((bf16[8,8,32,128]{3,2,1,0:T(8,128)(2,1)}), bf16[8,8,32,128]{3,2,1,0:T(8,128)(2,1)S(1)}, u32[]{:S(2)}, u32[]{:S(2)}) async-start(bf16[8,8,32,128]{3,2,1,0:T(8,128)(2,1)} %broadcast_in_dim.10), calls=%async_computation | async-start | bytes 1048576 | tf_op jit(solution)/shard_map/all_to_all | solution.py:295
  17.7 58.3 %copy-start.2 = (bf16[8,8,32,128]{3,2,1,0:T(8,128)(2,1)}, bf16[8,8,32,128]{3,2,1,0:T(8,128)(2,1)S(1)}, u32[]{:S(2)}) copy-start(bf16[8,8,32,128]{3,2,1,0:T(8,128)(2,1)S(1)} %all-to-all-done.args_1_) | copy-start | bytes 1572868
  130.5 17.3 %all-to-all-start.3 = ((bf16[8,9,32,128]{3,2,1,0:T(8,128)(2,1)}), bf16[8,9,32,128]{3,2,1,0:T(8,128)(2,1)S(1)}, u32[]{:S(2)}, u32[]{:S(2)}) async-start(bf16[8,9,32,128]{3,2,1,0:T(8,128)(2,1)} %get-tuple-element.10), calls=%async_computation.3 | async-start | bytes 1179648 | tf_op jit(solution)/shard_map/all_to_all | solution.py:308
  147.8 0.8 copy-start.1

commit v6 on v5

--- a/solution.py
+++ b/solution.py
@@ -94,7 +94,7 @@
 
 
 def hot_rows(row, wanted):
-    return jnp.where(row == wanted, 1.0, 0.0).astype(BF16)
+    return jnp.where(row.astype(BF16) == wanted.astype(BF16), BF16(1.0), BF16(0.0))
 
 
 def ctf_rows(index_rows, ctf_parts):
@@ -120,15 +120,22 @@
     return rows, ctf, scaled, rotations(rows, top, phases)
 
 
-def score_kernel(slabs, top, x_ref, refs_ref, ctf_parts, phases, prior_ref, me_ref, out_ref, table):
+def score_kernel(slabs, top, x_ref, refs_ref, ctf_parts, phases, prior_ref, me_ref, out_ref, table, stage, padded):
     half = slabs // 2
 
     @pl.when(pl.program_id(0) == 0)
     def _():
+        owned = stage.shape[0] // slabs
+        padded[...] = jnp.zeros_like(padded)
+        for dev in range(refs_ref.shape[0]):
+            stage[...] = refs_ref[dev].astype(F32)
+            for slab in range(slabs):
+                padded[slab, dev * 32 : dev * 32 + owned, :] = stage[pl.ds(slab, owned, stride=slabs), :]
         for slab in range(slabs):
+            rows = slice(slab * 128, (slab + 1) * 128)
             for piece in range(2):
-                devs = [refs_ref[piece * 4 + dev, slab].astype(F32) for dev in range(4)]
-                table[slab * 128 : (slab + 1) * 128, piece * 128 : (piece + 1) * 128] = jnp.concatenate(devs, axis=0).T.astype(BF16)
+                across = slice(piece * 128, (piece + 1) * 128)
+                table[rows, across] = padded[slab, across, :].T.astype(BF16)
 
     classes = row_iota(256).astype(F32)
 
@@ -163,18 +170,22 @@
     return pl.pallas_call(
         lambda *args: score_kernel(slabs, top, *args),
         name="score",
-        grid=(sources // 2,),
+        grid=(sources // 4,),
         in_specs=[
-            pl.BlockSpec((2, rows, lanes), lambda s: (s, 0, 0)),
+            pl.BlockSpec((4, rows, lanes), lambda s: (s, 0, 0)),
             whole(refs),
             whole(ctf_parts),
             whole(phases),
             whole(prior),
             pl.BlockSpec(memory_space=pltpu.SMEM),
         ],
-        out_specs=pl.BlockSpec((sources, 2, top, lanes), lambda s: (0, s, 0, 0)),
+        out_specs=pl.BlockSpec((sources, 4, top, lanes), lambda s: (0, s, 0, 0)),
         out_shape=jax.ShapeDtypeStruct((sources, sources, top, lanes), F32),
-        scratch_shapes=[pltpu.VMEM((slabs * 128, 256), BF16)],
+        scratch_shapes=[
+            pltpu.VMEM((slabs * 128, 256), BF16),
+            pltpu.VMEM(refs.shape[1:], F32),
+            pltpu.VMEM((slabs, 256, lanes), F32),
+        ],
         compiler_params=pltpu.CompilerParams(vmem_limit_bytes=VMEM_LIMIT),
     )(moved, refs, ctf_parts, phases, prior, me.astype(jnp.int32).reshape(1))
 
@@ -277,6 +288,8 @@
     return pl.pallas_call(
         lambda *args: finish_kernel(slabs, owned, *args),
         name="finish",
+        in_specs=[pl.BlockSpec(memory_space=pltpu.VMEM)],
+        out_specs=pl.BlockSpec(memory_space=pltpu.VMEM),
         out_shape=jax.ShapeDtypeStruct((owned, 2, slabs // 2, LANES), F32),
         compiler_params=pltpu.CompilerParams(vmem_limit_bytes=VMEM_LIMIT),
     )(parts)
@@ -290,7 +303,7 @@
     slabs = 2 * share
     me = lax.axis_index("dp")
 
-    own_refs = jnp.pad(references.transpose(1, 2, 0, 3).reshape(slabs, owned, harmonics), ((0, 0), (0, 32 - owned), (0, 0)))
+    own_refs = references.reshape(owned * slabs, harmonics)
     holders = lax.axis_size("cls")
     refs = lax.all_to_all(jnp.broadcast_to(own_refs[None], (holders,) + own_refs.shape), "cls", 0, 0)
     ctf = lax.dynamic_slice(ctf_table, (0, me * share), (ctf_table.shape[0], share)).T

time: 151 us -> 149 us (0.987)
  no operation moved by 1% of the time
where the time goes in v6:
time: 149 us
  blocking collectives  77 us (52%)
  Pallas kernels  42.7 us (29%)
  starting transfers between devices  12.9 us (9%)
  waiting for transfers between devices  10.9 us (7%)
  local copies, waits for them, and re-layouts  3.72 us (2%)
    all_to_all x1, blocking collectives, body(): moved = lax.all_to_all(send, 'dp', 0, 0)  58.3 us
    pallas_call x1, Pallas kernels, partial_scores(): pl.pallas_call(lambda *args: score_kernel(slabs, top, *args), name='score...  19.3 us
    all_to_all x1, blocking collectives, body(): partials = lax.all_to_all(partial, 'dp', 0, 0)  18.7 us
    pallas_call x1, Pallas kernels, weighted_sums(): pl.pallas_call(lambda *args: sum_kernel(slabs, top, *args), name='sums',...  15.9 us
    all_to_all x1, waiting for transfers between devices, body(): parts = lax.all_to_all(sums, 'cls', 0, 0)  8.92 us
    all_to_all x1, starting transfers between devices, body(): parts = lax.all_to_all(sums, 'cls', 0, 0)  7.13 us
    all_to_all x1, starting transfers between devices, body(): lax.all_to_all(jnp.broadcast_to(own_refs[None], (holders,) + own_refs.sha...  5.8 us
    pallas_call x1, Pallas kernels, cut_particles(): pl.pallas_call(lambda *refs: cut_kernel(share, owned, *refs), name='cut',...  5.61 us
  transfers between devices with their start and end apart: 2, of which 2 were waited for; matrix products, arithmetic and copies ran while one was open for 1% of the time, Pallas kernels for 4%

profile of v6, /device:TPU:1, one launch (start us, length us, event | category | flops | bytes accessed | tf_op | source)
XLA Modules:
  0.0 148.6 jit_solution(9375343651672797498)
XLA Ops:
  0.6 0.0 copy-start
  0.6 1.6 %broadcast_in_dim.12 = bf16[8,200,128]{2,1,0:T(8,128)(2,1)} broadcast(bf16[200,128]{1,0:T(8,128)(2,1)} %bitcast.12), dimensions={1,2} | broadcast | bytes 460800 | tf_op jit(solution)/shard_map/broadcast_in_dim | solution.py:308
  2.2 5.8 %all-to-all-start = ((bf16[8,200,128]{2,1,0:T(8,128)(2,1)}), bf16[8,200,128]{2,1,0:T(8,128)(2,1)S(1)}, u32[]{:S(2)}, u32[]{:S(2)}) async-start(bf16[8,200,128]{2,1,0:T(8,128)(2,1)} %broadcast_in_dim.12), calls=%async_computation | async-start | bytes 819200 | tf_op jit(solution)/shard_map/all_to_all | solution.py:308
  8.0 5.6 %cut.1 = bf16[16,1056,128]{2,1,0:T(8,128)(2,1)} custom-call(bf16[128,2,64,128]{3,2,1,0:T(8,128)(2,1)} %refs_0_.1, s32[8,128]{1,0:T(8,128)} %bitcast.13, s32[8,128]{1,0:T(8,128)} %bitcast.14, s32[1,128]{1,0:T(1,128)} %bitcast.16), custom_call_target="tpu_custom_call" | custom-call | bytes 8388608 | tf_op jit(solution)/shard_map/cut/pallas_call | solution.py:80
  13.7 0.0 copy-done
  13.7 0.6 pad_maximum_fusion.args_2_
  14.3 2.0 %all-to-all-done.args_1_ = bf16[8,200,128]{2,1,0:T(8,128)(2,1)S(1)} async-done(((bf16[8,200,128]{2,1,0:T(8,128)(2,1)}), bf16[8,200,128]{2,1,0:T(8,128)(2,1)S(1)}, u32[]{:S(2)}, u32[]{:S(2)}) %all-to-all-start) | async-done | bytes 409632 | tf_op jit(solution)/shard_map/all_to_all | solution.py:308
  16.3 0.0 copy-start.2
  16.3 58.3 %all_to_all.20.args_0_ = bf16[16,1056,128]{2,1,0:T(8,128)(2,1)} all-to-all(bf16[16,1056,128]{2,1,0:T(8,128)(2,1)} %cut.1), channel_id=1, replica_groups=mesh['dp'=16,'cls'=8] {'dp'}, dimensions={0} | all-to-all | bytes 8650752 | tf_op jit(solution)/shard_map/all_to_all | solution.py:316
  74.6 0.0 copy-done.2
  74.6 19.3 %score.1 = f32[16,16,8,128]{3,2,1,0:T(8,128)} custom-call(bf16[16,1056,128]{2,1,0:T(8,128)(2,1)} %all_to_all.20.args_0_, bf16[8,200,128]{2,1,0:T(8,128)(2,1)} %copy-done.2, bf16[24,128]{1,0:T(8,128)(2,1)} %pad_maximum_fusion.args_2_, bf16[256,128]{1,0:T(8,128)(2,1)} %constant.21.clone.args_3_, f32[8,128]{1,0:T(8,128)} %bitcast.15, s32[1]{0:T(128)} %bitcast.6.args_5_), custom_call_target="tpu_custom_call" | custom-call | tf_op jit(solution)/shard_map/score/pallas_call | solution.py:170
  94.0 18.7 %all_to_all.21.args_1_ = f32[16,16,8,128]{3,2,1,0:T(8,128)} all-to-all(f32[16,16,8,128]{3,2,1,0:T(8,128)} %score.1), channel_id=1, replica_groups=mesh['dp'=16,'cls'=8] {'dp'}, dimensions={0} | all-to-all | bytes 2097152 | tf_op jit(solution)/shard_map/all_to_all | solution.py:318
  112.7 15.9 %sums.1 = (f32[16,8,128]{2,1,0:T(8,128)}, bf16[8,9,32,128]{3,2,1,0:T(8,128)(2,1)}) custom-call(bf16[16,1056,128]{2,1,0:T(8,128)(2,1)} %all_to_all.20.args_0_, f32[16,16,8,128]{3,2,1,0:T(8,128)} %all_to_all.21.args_1_, bf16[24,128]{1,0:T(8,128)(2,1)} %pad_maximum_fusion.args_2_, bf16[256,128]{1,0:T(8,128)(2,1)} %constant.21.clone.args_3_), custom_call_target="tpu_custom_call" | custom-call | tf_op jit(solution)/shard_map/sums/pallas_call | solution.py:250
  128.5 7.1 %all-to-all-start.3 = ((bf16[8,9,32,128]{3,2,1,0:T(8,128)(2,1)}), bf16[8,9,32,128]{3,2,1,0:T(8,128)(2,1)S(1)}, u32[]{:S(2)}, u32[]{:S(2)}) async-start(bf16[8,9,32,128]{3,2,1,0:T(8,128)(2,1)} %get-tuple-element.10), calls=%async_computation.3 | async-start | bytes 1179648 | tf_op jit(solution)/shard_map/all_to_all | solution.py:321
  135.7 1.3 dynamic-slice_bitcast_fusion
  136.9 8.9 %all-to-all-done.3.args_0_ = bf16[8,9,32,128]{3,2,1,0:T(8,128)(2,1)S(1)} async-done(((bf16[8,9,32,128]{3,2,1,0:T(8,128)(2,1)}), bf16[8,9,32,128]{3,2,1,0:T(8,128)(2,1)S(1)}, u32[]{:S(2)}, u32[]{:S(2)}) %all-to-all-start.3) | async-done | bytes 589856 | tf_op jit(solution)/shard_map/all_to_all | solution.py:321
  145.9 0.0 copy-start.1
  145.9 0.8 copy-done.1
  146.7 1.9 %finish.1 = f32[25,2,4,128]{3,2,1,0:T(4,128)} custom-call(bf16[8,9,32,128]{3,2,1,0:T(8,128)(2,1)} %copy-done.1), custom_call_target="tpu_custom_call" | custom-call | tf_op jit(solution)/shard_map/finish/pallas_call | solution.py:288
  (2 shorter events, 0.0 us)
Async XLA Ops:
  0.6 13.0 %copy-start = (f32[128,64]{0,1:T(8,128)S(1)}, f32[128,64]{0,1:T(8,128)}, u32[]{:S(2)}) copy-start(f32[128,64]{0,1:T(8,128)} %param.14) | copy-start | bytes 98308
  2.2 14.1 %all-to-all-start = ((bf16[8,200,128]{2,1,0:T(8,128)(2,1)}), bf16[8,200,128]{2,1,0:T(8,128)(2,1)S(1)}, u32[]{:S(2)}, u32[]{:S(2)}) async-start(bf16[8,200,128]{2,1,0:T(8,128)(2,1)} %broadcast_in_dim.12), calls=%async_computation | async-start | bytes 819200 | tf_op jit(solution)/shard_map/all_to_all | solution.py:308
  16.3 58.3 %copy-start.2 = (bf16[8,200,128]{2,1,0:T(8,128)(2,1)}, bf16[8,200,128]{2,1,0:T(8,128)(2,1)S(1)}, u32[]{:S(2)}) copy-start(bf16[8,200,128]{2,1,0:T(8,128)(2,1)S(1)} %all-to-all-done.args_1_) | copy-start | bytes 1228804
  128.5 17.3 %all-to-all-start.3 = ((bf16[8,9,32,128]{3,2,1,0:T(8,128)(2,1)}), bf16[8,9,32,128]{3,2,1,0:T(8,128)(2,1)S(1)}, u32[]{:S(2)}, u32[]{:S(2)}) async-start(bf16[8,9,32,128]{3,2,1,0:T(8,128)(2,1)} %get-tuple-element.10), calls=%async_computation.3 | async-start | bytes 1179648 | tf_op jit(solution)/shard_map/all_to_all | solution.py:321
  145.9 0.8 copy-start.1

commit v7 on v6

--- a/solution.py
+++ b/solution.py
@@ -16,7 +16,7 @@
 BF16 = jnp.bfloat16
 LANES = 128
 INDEX_ROWS = 32
-VMEM_LIMIT = 56 * 1024 * 1024
+MIB = 1024 * 1024
 
 
 def split3_np(x):
@@ -85,7 +85,7 @@
         out_specs=pl.BlockSpec((owners, out_rows, lanes), lambda s: (0, 0, 0)),
         out_shape=jax.ShapeDtypeStruct((owners, out_rows, lanes), BF16),
         cost_estimate=pl.CostEstimate(flops=0, bytes_accessed=4 * particles.size, transcendentals=0),
-        compiler_params=pltpu.CompilerParams(vmem_limit_bytes=VMEM_LIMIT),
+        compiler_params=pltpu.CompilerParams(vmem_limit_bytes=56 * MIB),
     )(particles, classes, rotations, groups)
 
 
@@ -186,7 +186,7 @@
             pltpu.VMEM(refs.shape[1:], F32),
             pltpu.VMEM((slabs, 256, lanes), F32),
         ],
-        compiler_params=pltpu.CompilerParams(vmem_limit_bytes=VMEM_LIMIT),
+        compiler_params=pltpu.CompilerParams(vmem_limit_bytes=20 * MIB),
     )(moved, refs, ctf_parts, phases, prior, me.astype(jnp.int32).reshape(1))
 
 
@@ -263,7 +263,7 @@
         ],
         out_shape=[jax.ShapeDtypeStruct((sources, top, lanes), F32), jax.ShapeDtypeStruct(out, BF16)],
         scratch_shapes=[pltpu.VMEM((rows, 256), F32)],
-        compiler_params=pltpu.CompilerParams(vmem_limit_bytes=VMEM_LIMIT),
+        compiler_params=pltpu.CompilerParams(vmem_limit_bytes=32 * MIB),
     )(moved, partials, ctf_parts, phases)
 
 
@@ -291,7 +291,7 @@
         in_specs=[pl.BlockSpec(memory_space=pltpu.VMEM)],
         out_specs=pl.BlockSpec(memory_space=pltpu.VMEM),
         out_shape=jax.ShapeDtypeStruct((owned, 2, slabs // 2, LANES), F32),
-        compiler_params=pltpu.CompilerParams(vmem_limit_bytes=VMEM_LIMIT),
+        compiler_params=pltpu.CompilerParams(vmem_limit_bytes=6 * MIB),
     )(parts)
 
 

time: 149 us -> 143 us (0.960)
  Pallas kernels: 42.7 us -> 38.3 us
    pallas_call x1, Pallas kernels: 19.3 us -> 17.4 us  [partial_scores(): pl.pallas_call(lambda *args: score_kernel(slabs, top, *args), name='score...]
  transfers between devices with their start and end apart: 2 -> 2, of which waited for: 2 -> 2; matrix products, arithmetic and copies ran while one was open for 1% -> 0% of each run, Pallas kernels for 4% -> 4%
where the time goes in v7:
time: 143 us
  blocking collectives  77.2 us (54%)
  Pallas kernels  38.3 us (27%)
  starting transfers between devices  12.3 us (9%)
  waiting for transfers between devices  12.2 us (9%)
  local copies, waits for them, and re-layouts  2.25 us (2%)
    all_to_all x1, blocking collectives, body(): moved = lax.all_to_all(send, 'dp', 0, 0)  58.2 us
    all_to_all x1, blocking collectives, body(): partials = lax.all_to_all(partial, 'dp', 0, 0)  18.9 us
    pallas_call x1, Pallas kernels, partial_scores(): pl.pallas_call(lambda *args: score_kernel(slabs, top, *args), name='score...  17.4 us
    pallas_call x1, Pallas kernels, weighted_sums(): pl.pallas_call(lambda *args: sum_kernel(slabs, top, *args), name='sums',...  14.5 us
    all_to_all x1, waiting for transfers between devices, body(): parts = lax.all_to_all(sums, 'cls', 0, 0)  9.61 us
    all_to_all x1, starting transfers between devices, body(): parts = lax.all_to_all(sums, 'cls', 0, 0)  6.49 us
    all_to_all x1, starting transfers between devices, body(): lax.all_to_all(jnp.broadcast_to(own_refs[None], (holders,) + own_refs.sha...  5.8 us
    pallas_call x1, Pallas kernels, cut_particles(): pl.pallas_call(lambda *refs: cut_kernel(share, owned, *refs), name='cut',...  5.58 us
  transfers between devices with their start and end apart: 2, of which 2 were waited for; matrix products, arithmetic and copies ran while one was open for 0% of the time, Pallas kernels for 4%

profile of v7, /device:TPU:1, one launch (start us, length us, event | category | flops | bytes accessed | tf_op | source)
XLA Modules:
  0.0 142.9 jit_solution(5328611451420208158)
XLA Ops:
  0.6 0.0 copy-start
  0.6 1.6 %broadcast_in_dim.12 = bf16[8,200,128]{2,1,0:T(8,128)(2,1)} broadcast(bf16[200,128]{1,0:T(8,128)(2,1)} %bitcast.13), dimensions={1,2} | broadcast | bytes 460800 | tf_op jit(solution)/shard_map/broadcast_in_dim | solution.py:308
  2.3 5.8 %all-to-all-start = ((bf16[8,200,128]{2,1,0:T(8,128)(2,1)}), bf16[8,200,128]{2,1,0:T(8,128)(2,1)S(1)}, u32[]{:S(2)}, u32[]{:S(2)}) async-start(bf16[8,200,128]{2,1,0:T(8,128)(2,1)} %broadcast_in_dim.12), calls=%async_computation | async-start | bytes 819200 | tf_op jit(solution)/shard_map/all_to_all | solution.py:308
  8.1 5.6 %cut.1 = bf16[16,1056,128]{2,1,0:T(8,128)(2,1)} custom-call(bf16[128,2,64,128]{3,2,1,0:T(8,128)(2,1)} %refs_0_.1, s32[8,128]{1,0:T(8,128)} %bitcast.14, s32[8,128]{1,0:T(8,128)} %bitcast.15, s32[1,128]{1,0:T(1,128)} %bitcast.16), custom_call_target="tpu_custom_call" | custom-call | bytes 8388608 | tf_op jit(solution)/shard_map/cut/pallas_call | solution.py:80
  13.7 0.0 copy-done
  13.7 0.0 copy-start.1
  13.7 0.0 copy-start.2
  13.7 2.6 %all-to-all-done.args_1_ = bf16[8,200,128]{2,1,0:T(8,128)(2,1)S(1)} async-done(((bf16[8,200,128]{2,1,0:T(8,128)(2,1)}), bf16[8,200,128]{2,1,0:T(8,128)(2,1)S(1)}, u32[]{:S(2)}, u32[]{:S(2)}) %all-to-all-start) | async-done | bytes 409632 | tf_op jit(solution)/shard_map/all_to_all | solution.py:308
  16.3 58.2 %all_to_all.20.args_0_ = bf16[16,1056,128]{2,1,0:T(8,128)(2,1)S(1)} all-to-all(bf16[16,1056,128]{2,1,0:T(8,128)(2,1)} %cut.1), channel_id=1, replica_groups=mesh['dp'=16,'cls'=8] {'dp'}, dimensions={0} | all-to-all | bytes 8650752 | tf_op jit(solution)/shard_map/all_to_all | solution.py:316
  74.6 0.0 copy-done.1
  74.6 0.0 copy-done.2
  74.6 17.4 %score.1 = f32[16,16,8,128]{3,2,1,0:T(8,128)S(1)} custom-call(bf16[16,1056,128]{2,1,0:T(8,128)(2,1)S(1)} %all_to_all.20.args_0_, bf16[8,200,128]{2,1,0:T(8,128)(2,1)S(1)} %all-to-all-done.args_1_, bf16[24,128]{1,0:T(8,128)(2,1)S(1)} %pad_maximum_fusion.args_2_, bf16[256,128]{1,0:T(8,128)(2,1)S(1)} %copy-done.1, f32[8,128]{1,0:T(8,128)S(1)} %bitcast.12, ...), custom_call_target="tpu_custom_call" | custom-call | tf_op jit(solution)/shard_map/score/pallas_call | solution.py:170
  91.9 18.9 %all_to_all.21.args_1_ = f32[16,16,8,128]{3,2,1,0:T(8,128)S(1)} all-to-all(f32[16,16,8,128]{3,2,1,0:T(8,128)S(1)} %score.1), channel_id=1, replica_groups=mesh['dp'=16,'cls'=8] {'dp'}, dimensions={0} | all-to-all | bytes 2097152 | tf_op jit(solution)/shard_map/all_to_all | solution.py:318
  110.9 14.5 %sums.1 = (f32[16,8,128]{2,1,0:T(8,128)S(1)}, bf16[8,9,32,128]{3,2,1,0:T(8,128)(2,1)}) custom-call(bf16[16,1056,128]{2,1,0:T(8,128)(2,1)S(1)} %all_to_all.20.args_0_, f32[16,16,8,128]{3,2,1,0:T(8,128)S(1)} %all_to_all.21.args_1_, bf16[24,128]{1,0:T(8,128)(2,1)S(1)} %pad_maximum_fusion.args_2_, bf16[256,128]{1,0:T(8,128)(2,1)S(1)} %copy-done.1), custom_call_target="tpu_custom_call" | custom-call | tf_op jit(solution)/shard_map/sums/pallas_call | solution.py:250
  125.4 6.5 %all-to-all-start.3 = ((bf16[8,9,32,128]{3,2,1,0:T(8,128)(2,1)}), bf16[8,9,32,128]{3,2,1,0:T(8,128)(2,1)S(1)}, u32[]{:S(2)}, u32[]{:S(2)}) async-start(bf16[8,9,32,128]{3,2,1,0:T(8,128)(2,1)} %get-tuple-element.10), calls=%async_computation.3 | async-start | bytes 1179648 | tf_op jit(solution)/shard_map/all_to_all | solution.py:321
  131.9 0.6 dynamic-slice_bitcast_fusion
  132.5 9.6 %all-to-all-done.3.args_0_ = bf16[8,9,32,128]{3,2,1,0:T(8,128)(2,1)S(1)} async-done(((bf16[8,9,32,128]{3,2,1,0:T(8,128)(2,1)}), bf16[8,9,32,128]{3,2,1,0:T(8,128)(2,1)S(1)}, u32[]{:S(2)}, u32[]{:S(2)}) %all-to-all-start.3) | async-done | bytes 589856 | tf_op jit(solution)/shard_map/all_to_all | solution.py:321
  142.1 0.9 finish.1
  (3 shorter events, 0.0 us)
Async XLA Ops:
  0.6 13.0 %copy-start = (f32[128,64]{0,1:T(8,128)S(1)}, f32[128,64]{0,1:T(8,128)}, u32[]{:S(2)}) copy-start(f32[128,64]{0,1:T(8,128)} %param.14) | copy-start | bytes 98308
  2.3 14.1 %all-to-all-start = ((bf16[8,200,128]{2,1,0:T(8,128)(2,1)}), bf16[8,200,128]{2,1,0:T(8,128)(2,1)S(1)}, u32[]{:S(2)}, u32[]{:S(2)}) async-start(bf16[8,200,128]{2,1,0:T(8,128)(2,1)} %broadcast_in_dim.12), calls=%async_computation | async-start | bytes 819200 | tf_op jit(solution)/shard_map/all_to_all | solution.py:308
  13.7 60.9 %copy-start.1 = (bf16[256,128]{1,0:T(8,128)(2,1)S(1)}, bf16[256,128]{1,0:T(8,128)(2,1)}, u32[]{:S(2)}) copy-start(bf16[256,128]{1,0:T(8,128)(2,1)} %constant.21.clone.args_3_) | copy-start | bytes 196612
  13.7 60.8 %copy-start.2 = (f32[128,8]{0,1:T(8,128)S(1)}, f32[128,8]{0,1:T(8,128)}, u32[]{:S(2)}) copy-start(f32[128,8]{0,1:T(8,128)} %param.13) | copy-start | bytes 12292
  125.4 16.7 %all-to-all-start.3 = ((bf16[8,9,32,128]{3,2,1,0:T(8,128)(2,1)}), bf16[8,9,32,128]{3,2,1,0:T(8,128)(2,1)S(1)}, u32[]{:S(2)}, u32[]{:S(2)}) async-start(bf16[8,9,32,128]{3,2,1,0:T(8,128)(2,1)} %get-tuple-element.10), calls=%async_computation.3 | async-start | bytes 1179648 | tf_op jit(solution)/shard_map/all_to_all | solution.py:321

commit v8 on v7

--- a/solution.py
+++ b/solution.py
@@ -139,8 +139,9 @@
 
     classes = row_iota(256).astype(F32)
 
-    for s in range(x_ref.shape[0]):
-        index, _, scaled, angles = prepared(s, slabs, top, x_ref, ctf_parts, phases)
+    base = pl.program_id(0) * out_ref.shape[1]
+    for s in range(out_ref.shape[1]):
+        index, _, scaled, angles = prepared(base + s, slabs, top, x_ref, ctf_parts, phases)
         scores = []
         for pair in range(top // 2):
             hot = jnp.concatenate([hot_rows(index[j : j + 1, :], classes) for j in (2 * pair, 2 * pair + 1)], axis=1)
@@ -158,7 +159,7 @@
             for side in range(2):
                 across = slice((2 * pair + side) * 128, (2 * pair + side + 1) * 128)
                 scores.append(jnp.sum(angles[:128, across] * evens[side] + angles[128:, across] * odds[side], axis=0, keepdims=True))
-        own = pl.program_id(0) * x_ref.shape[0] + s == me_ref[0]
+        own = base + s == me_ref[0]
         score = SCORE_SCALE * jnp.concatenate(scores, axis=0) + jnp.where(own, prior_ref[...], 0.0)
         for owner in range(out_ref.shape[0]):
             out_ref[owner, s] = score
@@ -172,7 +173,7 @@
         name="score",
         grid=(sources // 4,),
         in_specs=[
-            pl.BlockSpec((4, rows, lanes), lambda s: (s, 0, 0)),
+            pl.BlockSpec(memory_space=pltpu.VMEM),
             whole(refs),
             whole(ctf_parts),
             whole(phases),
@@ -212,8 +213,9 @@
     raised = jnp.exp(score - jnp.max(score, axis=1, keepdims=True))
     weights = raised / jnp.sum(raised, axis=1, keepdims=True)
     parts, hots = [], []
-    for s in range(x_ref.shape[0]):
-        index, ctf, scaled, angles = prepared(s, slabs, top, x_ref, ctf_parts, phases)
+    base = step * weight_ref.shape[0]
+    for s in range(weight_ref.shape[0]):
+        index, ctf, scaled, angles = prepared(base + s, slabs, top, x_ref, ctf_parts, phases)
         squared = ctf * ctf
         weight = weights[s]
         for pair in range(top // 2):
@@ -252,7 +254,7 @@
         name="sums",
         grid=(sources // 4,),
         in_specs=[
-            pl.BlockSpec((4, rows, lanes), lambda s: (s, 0, 0)),
+            pl.BlockSpec(memory_space=pltpu.VMEM),
             pl.BlockSpec((sources, 4, top, lanes), lambda s: (0, s, 0, 0)),
             whole(ctf_parts),
             whole(phases),

time: 143 us -> 143 us (level)
  no operation moved by 1% of the time
where the time goes in v8:
time: 143 us
  blocking collectives  77.1 us (54%)
  Pallas kernels  38.2 us (27%)
  starting transfers between devices  12.3 us (9%)
  waiting for transfers between devices  12.2 us (9%)
  local copies, waits for them, and re-layouts  2.25 us (2%)
    all_to_all x1, blocking collectives, body(): moved = lax.all_to_all(send, 'dp', 0, 0)  58.2 us
    all_to_all x1, blocking collectives, body(): partials = lax.all_to_all(partial, 'dp', 0, 0)  18.9 us
    pallas_call x1, Pallas kernels, partial_scores(): pl.pallas_call(lambda *args: score_kernel(slabs, top, *args), name='score...  17.2 us
    pallas_call x1, Pallas kernels, weighted_sums(): pl.pallas_call(lambda *args: sum_kernel(slabs, top, *args), name='sums',...  14.5 us
    all_to_all x1, waiting for transfers between devices, body(): parts = lax.all_to_all(sums, 'cls', 0, 0)  9.61 us
    all_to_all x1, starting transfers between devices, body(): parts = lax.all_to_all(sums, 'cls', 0, 0)  6.5 us
    all_to_all x1, starting transfers between devices, body(): lax.all_to_all(jnp.broadcast_to(own_refs[None], (holders,) + own_refs.sha...  5.8 us
    pallas_call x1, Pallas kernels, cut_particles(): pl.pallas_call(lambda *refs: cut_kernel(share, owned, *refs), name='cut',...  5.58 us
  transfers between devices with their start and end apart: 2, of which 2 were waited for; matrix products, arithmetic and copies ran while one was open for 0% of the time, Pallas kernels for 4%

profile of v8, /device:TPU:1, one launch (start us, length us, event | category | flops | bytes accessed | tf_op | source)
XLA Modules:
  0.0 142.8 jit_solution(3549359019817359307)
XLA Ops:
  0.6 0.0 copy-start
  0.6 1.6 %broadcast_in_dim.12 = bf16[8,200,128]{2,1,0:T(8,128)(2,1)} broadcast(bf16[200,128]{1,0:T(8,128)(2,1)} %bitcast.13), dimensions={1,2} | broadcast | bytes 460800 | tf_op jit(solution)/shard_map/broadcast_in_dim | solution.py:310
  2.3 5.8 %all-to-all-start = ((bf16[8,200,128]{2,1,0:T(8,128)(2,1)}), bf16[8,200,128]{2,1,0:T(8,128)(2,1)S(1)}, u32[]{:S(2)}, u32[]{:S(2)}) async-start(bf16[8,200,128]{2,1,0:T(8,128)(2,1)} %broadcast_in_dim.12), calls=%async_computation | async-start | bytes 819200 | tf_op jit(solution)/shard_map/all_to_all | solution.py:310
  8.1 5.6 %cut.1 = bf16[16,1056,128]{2,1,0:T(8,128)(2,1)} custom-call(bf16[128,2,64,128]{3,2,1,0:T(8,128)(2,1)} %refs_0_.1, s32[8,128]{1,0:T(8,128)} %bitcast.14, s32[8,128]{1,0:T(8,128)} %bitcast.15, s32[1,128]{1,0:T(1,128)} %bitcast.16), custom_call_target="tpu_custom_call" | custom-call | bytes 8388608 | tf_op jit(solution)/shard_map/cut/pallas_call | solution.py:80
  13.7 0.0 copy-done
  13.7 0.0 copy-start.1
  13.7 0.0 copy-start.2
  13.7 2.6 %all-to-all-done.args_1_ = bf16[8,200,128]{2,1,0:T(8,128)(2,1)S(1)} async-done(((bf16[8,200,128]{2,1,0:T(8,128)(2,1)}), bf16[8,200,128]{2,1,0:T(8,128)(2,1)S(1)}, u32[]{:S(2)}, u32[]{:S(2)}) %all-to-all-start) | async-done | bytes 409632 | tf_op jit(solution)/shard_map/all_to_all | solution.py:310
  16.3 58.2 %all_to_all.20.args_0_ = bf16[16,1056,128]{2,1,0:T(8,128)(2,1)S(1)} all-to-all(bf16[16,1056,128]{2,1,0:T(8,128)(2,1)} %cut.1), channel_id=1, replica_groups=mesh['dp'=16,'cls'=8] {'dp'}, dimensions={0} | all-to-all | bytes 8650752 | tf_op jit(solution)/shard_map/all_to_all | solution.py:318
  74.6 0.0 copy-done.1
  74.6 0.0 copy-done.2
  74.6 17.2 %score.1 = f32[16,16,8,128]{3,2,1,0:T(8,128)S(1)} custom-call(bf16[16,1056,128]{2,1,0:T(8,128)(2,1)S(1)} %all_to_all.20.args_0_, bf16[8,200,128]{2,1,0:T(8,128)(2,1)S(1)} %all-to-all-done.args_1_, bf16[24,128]{1,0:T(8,128)(2,1)S(1)} %pad_maximum_fusion.args_2_, bf16[256,128]{1,0:T(8,128)(2,1)S(1)} %copy-done.1, f32[8,128]{1,0:T(8,128)S(1)} %bitcast.12, ...), custom_call_target="tpu_custom_call" | custom-call | tf_op jit(solution)/shard_map/score/pallas_call | solution.py:171
  91.8 18.9 %all_to_all.21.args_1_ = f32[16,16,8,128]{3,2,1,0:T(8,128)S(1)} all-to-all(f32[16,16,8,128]{3,2,1,0:T(8,128)S(1)} %score.1), channel_id=1, replica_groups=mesh['dp'=16,'cls'=8] {'dp'}, dimensions={0} | all-to-all | bytes 2097152 | tf_op jit(solution)/shard_map/all_to_all | solution.py:320
  110.7 14.5 %sums.1 = (f32[16,8,128]{2,1,0:T(8,128)S(1)}, bf16[8,9,32,128]{3,2,1,0:T(8,128)(2,1)}) custom-call(bf16[16,1056,128]{2,1,0:T(8,128)(2,1)S(1)} %all_to_all.20.args_0_, f32[16,16,8,128]{3,2,1,0:T(8,128)S(1)} %all_to_all.21.args_1_, bf16[24,128]{1,0:T(8,128)(2,1)S(1)} %pad_maximum_fusion.args_2_, bf16[256,128]{1,0:T(8,128)(2,1)S(1)} %copy-done.1), custom_call_target="tpu_custom_call" | custom-call | tf_op jit(solution)/shard_map/sums/pallas_call | solution.py:252
  125.2 6.5 %all-to-all-start.3 = ((bf16[8,9,32,128]{3,2,1,0:T(8,128)(2,1)}), bf16[8,9,32,128]{3,2,1,0:T(8,128)(2,1)S(1)}, u32[]{:S(2)}, u32[]{:S(2)}) async-start(bf16[8,9,32,128]{3,2,1,0:T(8,128)(2,1)} %get-tuple-element.10), calls=%async_computation.3 | async-start | bytes 1179648 | tf_op jit(solution)/shard_map/all_to_all | solution.py:323
  131.7 0.6 dynamic-slice_bitcast_fusion
  132.3 9.6 %all-to-all-done.3.args_0_ = bf16[8,9,32,128]{3,2,1,0:T(8,128)(2,1)S(1)} async-done(((bf16[8,9,32,128]{3,2,1,0:T(8,128)(2,1)}), bf16[8,9,32,128]{3,2,1,0:T(8,128)(2,1)S(1)}, u32[]{:S(2)}, u32[]{:S(2)}) %all-to-all-start.3) | async-done | bytes 589856 | tf_op jit(solution)/shard_map/all_to_all | solution.py:323
  141.9 0.9 finish.1
  (3 shorter events, 0.0 us)
Async XLA Ops:
  0.6 13.0 %copy-start = (f32[128,64]{0,1:T(8,128)S(1)}, f32[128,64]{0,1:T(8,128)}, u32[]{:S(2)}) copy-start(f32[128,64]{0,1:T(8,128)} %param.14) | copy-start | bytes 98308
  2.3 14.1 %all-to-all-start = ((bf16[8,200,128]{2,1,0:T(8,128)(2,1)}), bf16[8,200,128]{2,1,0:T(8,128)(2,1)S(1)}, u32[]{:S(2)}, u32[]{:S(2)}) async-start(bf16[8,200,128]{2,1,0:T(8,128)(2,1)} %broadcast_in_dim.12), calls=%async_computation | async-start | bytes 819200 | tf_op jit(solution)/shard_map/all_to_all | solution.py:310
  13.7 60.9 %copy-start.1 = (bf16[256,128]{1,0:T(8,128)(2,1)S(1)}, bf16[256,128]{1,0:T(8,128)(2,1)}, u32[]{:S(2)}) copy-start(bf16[256,128]{1,0:T(8,128)(2,1)} %constant.21.clone.args_3_) | copy-start | bytes 196612
  13.7 60.8 %copy-start.2 = (f32[128,8]{0,1:T(8,128)S(1)}, f32[128,8]{0,1:T(8,128)}, u32[]{:S(2)}) copy-start(f32[128,8]{0,1:T(8,128)} %param.13) | copy-start | bytes 12292
  125.2 16.7 %all-to-all-start.3 = ((bf16[8,9,32,128]{3,2,1,0:T(8,128)(2,1)}), bf16[8,9,32,128]{3,2,1,0:T(8,128)(2,1)S(1)}, u32[]{:S(2)}, u32[]{:S(2)}) async-start(bf16[8,9,32,128]{3,2,1,0:T(8,128)(2,1)} %get-tuple-element.10), calls=%async_computation.3 | async-start | bytes 1179648 | tf_op jit(solution)/shard_map/all_to_all | solution.py:323
